TPU v7x, 128 devices: a whole 4x4x4 slice. The times are simulated.
128 devices in a mesh: row: 32 (over x, z, core), col: 4 (over y).
Axes of the slice: x: 4, y: 4, z: 4, core: 2. Of those that a mesh axis runs over, the one named last changes fastest.
Arguments:
- panel: float32 [24576, 1536], P('row', 'col'), as said below
- trailing: float32 [24576, 3072], P('row', 'col'), may hold values from -6 to 6
- child_tiles: float32 [16384, 128, 128], P(('row', 'col')), may hold values from -6 to 6
- child_owner: int32 [16384], P(('row', 'col')), may hold values from 0 to 127, as said below
- child_tile: int32 [16384], P(('row', 'col')), may hold values from 0 to 35
- child_rows: int32 [16384, 128], P(('row', 'col')), may hold values from 0 to 127, each once within a row
Outputs:
- factor_panel: float32 [24576, 1536], P('row', 'col')
- new_trailing: float32 [24576, 3072], P('row', 'col')
Inputs may be any that keep to these rules, and one draw needn't show every extreme that they name: `panel`: the symmetric part of the first 1536 rows is positive definite. `child_owner`: the 128 tiles of one device name every owner at most 2 times; one owner, drawn from the seed, is named exactly 2 times by every device.
All inputs are finite; a program needn't handle non-finite values.
Results may differ from a plain program's by a relative error of at most 0.000057.
Values sent between devices are 32-bit elements; how exact they have to be, the bound alone decides.
A program may use at most 256 MiB of HBM per device.

v0:
```python
import jax
import jax.numpy as jnp
from jax import lax
from jax.sharding import PartitionSpec as P

PW = 1536


def from_root(value, axis, source):
    kept = jnp.where(lax.axis_index(axis) == source, value, 0).astype(value.dtype)
    return lax.psum(kept, axis)


def rank_within(owner_ids):
    tile_count = owner_ids.shape[0]
    same_owner = owner_ids[:, None] == owner_ids[None, :]
    positions = jnp.arange(tile_count, dtype=jnp.int32)
    earlier = positions[None, :] < positions[:, None]
    return jnp.sum(same_owner & earlier, axis=1)


def body(panel, trailing, child_tiles, child_owner, child_tile, child_rows):
    row_devices = lax.axis_size("row")
    col_devices = lax.axis_size("col")
    device_count = row_devices * col_devices
    tile_size = child_tiles.shape[1]
    capacity = max(2, 2 * child_tiles.shape[0] // device_count)
    slot_index = rank_within(child_owner)
    send_tiles = jnp.zeros((device_count, capacity, tile_size, tile_size), jnp.float32)
    send_tiles = send_tiles.at[child_owner, slot_index].set(child_tiles)
    send_rows = jnp.zeros((device_count, capacity, tile_size), jnp.int32)
    send_rows = send_rows.at[child_owner, slot_index].set(child_rows)
    send_target = jnp.full((device_count, capacity), -1, jnp.int32)
    send_target = send_target.at[child_owner, slot_index].set(child_tile)
    got_tiles, got_rows, got_target = (
        lax.all_to_all(send_tiles, ("row", "col"), split_axis=0, concat_axis=0, tiled=True),
        lax.all_to_all(send_rows, ("row", "col"), split_axis=0, concat_axis=0, tiled=True),
        lax.all_to_all(send_target, ("row", "col"), split_axis=0, concat_axis=0, tiled=True),
    )
    got_tiles = got_tiles.reshape(-1, tile_size, tile_size)
    got_rows = got_rows.reshape(-1, tile_size)
    got_target = got_target.reshape(-1)
    is_valid = got_target >= 0
    target = jnp.maximum(got_target, 0)
    row_count = trailing.shape[0]
    trail_cols = trailing.shape[1]
    tile_cols = trail_cols // tile_size
    tile_row = target // tile_cols
    tile_col = target % tile_cols
    blocked = trailing.reshape(row_count // tile_size, tile_size, tile_cols, tile_size)
    blocked = blocked.at[tile_row[:, None], got_rows, tile_col[:, None]].add(
        jnp.where(is_valid[:, None, None], got_tiles, 0.0)
    )
    assembled = blocked.reshape(row_count, trail_cols)
    panel_cols = panel.shape[1]
    row_index = lax.axis_index("row")
    col_index = lax.axis_index("col")
    block_total = max(PW // row_count, 1)
    diag_pieces = [from_root(panel, "row", block_index) for block_index in range(block_total)]
    diag_slab = jnp.concatenate(diag_pieces, axis=0)
    diag_block = lax.all_gather(diag_slab, "col", axis=1, tiled=True)
    diagonal_factor = jnp.linalg.cholesky(diag_block)
    full_rows = lax.all_gather(panel, "col", axis=1, tiled=True)
    solved = jax.scipy.linalg.solve_triangular(diagonal_factor, full_rows.T, lower=True).T
    global_row = row_index * row_count + jnp.arange(row_count, dtype=jnp.int32)
    padded_diag = jnp.concatenate(
        [diagonal_factor, jnp.zeros((row_count, PW), jnp.float32)], axis=0
    )
    diag_rows = lax.dynamic_slice_in_dim(
        padded_diag, jnp.minimum(row_index * row_count, PW), row_count, 0
    )
    factor_rows = jnp.where(global_row[:, None] < PW, diag_rows, solved)
    factor_panel = lax.dynamic_slice_in_dim(factor_rows, col_index * panel_cols, panel_cols, 1)
    first_row = PW + col_index * trail_cols
    first_owner = first_row // row_count
    brought = from_root(factor_rows, "row", first_owner + 0)
    product = lax.dot_general(
        factor_rows, brought, (((1,), (1,)), ((), ())), precision=lax.Precision.HIGHEST
    )
    new_trailing = assembled - jnp.where(global_row[:, None] >= PW, product, 0.0)
    return (factor_panel, new_trailing)


def solution(mesh):
    in_specs = (
        P("row", "col"),
        P("row", "col"),
        P(("row", "col"), None, None),
        P(("row", "col")),
        P(("row", "col")),
        P(("row", "col"), None),
    )
    out_specs = (P("row", "col"), P("row", "col"))
    return jax.shard_map(body, mesh=mesh, in_specs=in_specs, out_specs=out_specs, check_vma=False)
```

profile of v0, /device:TPU:26, one launch (start us, length us, event | category | flops | bytes accessed | tf_op | source)
XLA Modules:
  0.0 1081.1 jit_solution(8416870992163217531)
XLA Ops:
  10.6 110.6 %all-reduce.8.cloned.1.call-done = (f32[768,384]{0,1:T(8,128)}, f32[768,384]{0,1:T(8,128)}) async-done(((f32[768,384]{0,1:T(8,128)}, f32[768,384]{0,1:T(8,128)}), (f32[768,384]{0,1:T(8,128)}, f32[768,384]{0,1:T(8,128)})) %all-reduce.8.cloned.1.call-update) | async-done | bytes 2359312 | tf_op jit(solution)/shard_map/psum | solution.py:11
  121.3 3.3 pad_maximum_fusion
  125.5 6.4 scatter_fusion
  132.6 8.3 all-to-all-start
  141.6 3.8 reshape.244
  148.4 13.2 %scatter_fusion.1 = s32[128,2,128]{2,1,0:T(2,128)} fusion(s32[128,2,128]{2,1,0:T(2,128)} %broadcast_in_dim.86, s32[128]{0:T(128)S(1)} %fusion.127, s32[128,128]{1,0:T(8,128)S(1)} %copy-done.14), kind=kCustom, calls=%fused_computation.1 | custom fusion | bytes 197632 | tf_op jit(solution)/shard_map/scatter | solution.py:32
  161.6 7.9 broadcast_in_dim.89
  169.4 24.8 %scatter_fusion.2 = f32[128,2,128,128]{3,2,1,0:T(8,128)} fusion(f32[128,2,128,128]{3,2,1,0:T(8,128)} %broadcast_in_dim.89, s32[128]{0:T(128)S(1)} %fusion.127, f32[128,128,128]{2,1,0:T(8,128)} %param.8), kind=kCustom, calls=%fused_computation.2 | custom fusion | bytes 25166848 | tf_op jit(solution)/shard_map/scatter | solution.py:30
  194.3 9.8 all-to-all-start.1
  205.8 5.9 all-to-all-done.1
  211.7 7.8 all-to-all-start.2
  221.2 9.7 copy.65
  230.9 13.2 %fusion = f32[1536,1536]{1,0:T(8,128)} fusion(f32[1536,1536]{1,0:T(8,128)} %copy.65, f32[1536,1536]{0,1:T(8,128)} %all-gather.3.cloned.1.call-done), kind=kLoop, calls=%fused_computation.9 | loop fusion | flops 4718592 | bytes 28311552 | tf_op jit(solution)/shard_map/jit(cholesky)/div | solution.py:62
  245.0 11.7 %cholesky.343 = f32[128,128]{1,0:T(8,128)S(1)} custom-call(f32[128,128]{1,0:T(8,128)S(1)} %cholesky.898), custom_call_target="Cholesky" | custom-call | tf_op jit(solution)/shard_map/jit(cholesky)/cholesky | solution.py:62
  256.7 4.8 cholesky.373
  261.6 9.8 custom-call.95
  276.0 11.9 %cholesky.364 = f32[128,128]{1,0:T(8,128)S(1)} custom-call(f32[128,128]{1,0:T(8,128)S(1)} %cholesky.902), custom_call_target="Cholesky" | custom-call | tf_op jit(solution)/shard_map/jit(cholesky)/cholesky | solution.py:62
  288.6 9.8 custom-call.96
  302.7 11.7 %cholesky.389 = f32[128,128]{1,0:T(8,128)S(1)} custom-call(f32[128,128]{1,0:T(8,128)S(1)} %cholesky.907), custom_call_target="Cholesky" | custom-call | tf_op jit(solution)/shard_map/jit(cholesky)/cholesky | solution.py:62
  315.8 10.2 custom-call.97
  327.6 3.3 convolution_subtract_fusion
  331.0 11.7 %cholesky.719 = f32[128,128]{1,0:T(8,128)S(1)} custom-call(f32[128,128]{1,0:T(8,128)S(1)} %cholesky.912), custom_call_target="Cholesky" | custom-call | tf_op jit(solution)/shard_map/jit(cholesky)/cholesky | solution.py:62
  344.0 9.8 custom-call.98
  355.2 3.6 fusion.27
  358.8 11.9 %cholesky.738 = f32[128,128]{1,0:T(8,128)S(1)} custom-call(f32[128,128]{1,0:T(8,128)S(1)} %cholesky.917), custom_call_target="Cholesky" | custom-call | tf_op jit(solution)/shard_map/jit(cholesky)/cholesky | solution.py:62
  372.0 9.8 custom-call.99
  383.1 3.8 fusion.30
  387.0 11.7 %cholesky.758 = f32[128,128]{1,0:T(8,128)S(1)} custom-call(f32[128,128]{1,0:T(8,128)S(1)} %cholesky.922), custom_call_target="Cholesky" | custom-call | tf_op jit(solution)/shard_map/jit(cholesky)/cholesky | solution.py:62
  400.0 10.0 custom-call.100
  411.3 3.8 fusion.36
  415.1 11.7 %cholesky.778 = f32[128,128]{1,0:T(8,128)S(1)} custom-call(f32[128,128]{1,0:T(8,128)S(1)} %cholesky.927), custom_call_target="Cholesky" | custom-call | tf_op jit(solution)/shard_map/jit(cholesky)/cholesky | solution.py:62
  427.5 9.8 custom-call.101
  438.5 4.2 fusion.39
  442.7 11.7 %cholesky.798 = f32[128,128]{1,0:T(8,128)S(1)} custom-call(f32[128,128]{1,0:T(8,128)S(1)} %cholesky.932), custom_call_target="Cholesky" | custom-call | tf_op jit(solution)/shard_map/jit(cholesky)/cholesky | solution.py:62
  455.1 9.8 custom-call.102
  466.0 3.6 fusion.47
  469.6 11.9 %cholesky.818 = f32[128,128]{1,0:T(8,128)S(1)} custom-call(f32[128,128]{1,0:T(8,128)S(1)} %cholesky.937), custom_call_target="Cholesky" | custom-call | tf_op jit(solution)/shard_map/jit(cholesky)/cholesky | solution.py:62
  482.1 9.8 custom-call.103
  492.9 3.3 fusion.50
  496.3 11.7 %cholesky.838 = f32[128,128]{1,0:T(8,128)S(1)} custom-call(f32[128,128]{1,0:T(8,128)S(1)} %cholesky.942), custom_call_target="Cholesky" | custom-call | tf_op jit(solution)/shard_map/jit(cholesky)/cholesky | solution.py:62
  508.6 9.8 custom-call.104
  522.1 12.1 %cholesky.858 = f32[128,128]{1,0:T(8,128)S(1)} custom-call(f32[128,128]{1,0:T(8,128)S(1)} %cholesky.947), custom_call_target="Cholesky" | custom-call | tf_op jit(solution)/shard_map/jit(cholesky)/cholesky | solution.py:62
  534.9 9.8 custom-call.105
  549.1 11.7 %cholesky.876 = f32[128,128]{1,0:T(8,128)S(1)} custom-call(f32[128,128]{1,0:T(8,128)S(1)} %convolution_subtract_fusion.13), custom_call_target="Cholesky" | custom-call | tf_op jit(solution)/shard_map/jit(cholesky)/cholesky | solution.py:62
  572.5 12.9 %fusion.1 = (f32[1536,1536]{1,0:T(8,128)}, f32[1536,1536]{1,0:T(8,128)}) fusion(f32[1536,1536]{1,0:T(8,128)} %get-tuple-element.88, pred[]{:T(512)S(6)} %cholesky.897), kind=kLoop, calls=%fused_computation.12 | loop fusion | flops 9437184 | bytes 28311552 | tf_op jit(solution)/shard_map/jit(_solve_triangular)/triangular_solve | solution.py:64
  585.4 43.4 %while.1 = (s32[]{:T(128)}, f32[1536,1536]{1,0:T(8,128)}, s32[12,2]{0,1:T(2,128)S(1)}, f32[12,128,128]{2,1,0:T(8,128)}, s32[]{:T(128)}) while((s32[]{:T(128)}, f32[1536,1536]{1,0:T(8,128)}, s32[12,2]{0,1:T(2,128)S(1)}, f32[12,128,128]{2,1,0:T(8,128)}, s32[]{:T(128)}) %tuple.109), condition=%wide.while_cond, body=%wide.while_body.sunk | while | flops 2 | bytes 132705 | solution.py:64
  615.1 3.0 bitcast_dynamic-update-slice_fusion.2
  628.8 118.7 %custom-call.106 = f32[12,128,128]{1,2,0:T(8,128)S(1)} custom-call(f32[12,128,128]{2,1,0:T(8,128)} %get-tuple-element.9), custom_call_target="InvertDiagBlocksLowerTriangular" | custom-call | tf_op jit(solution)/shard_map/jit(_solve_triangular)/triangular_solve | solution.py:64
  747.6 3.5 constant_dynamic-update-slice_fusion.55
  753.5 3.1 constant_dynamic-update-slice_fusion.54
  759.2 3.1 constant_dynamic-update-slice_fusion.53
  765.2 3.2 constant_dynamic-update-slice_fusion.52
  772.6 3.2 constant_dynamic-update-slice_fusion.51
  775.8 3.0 convolution_subtract_fusion.4
  781.1 3.2 convolution_subtract_fusion.10
  786.4 3.7 convolution_subtract_fusion.3
  792.4 4.1 convolution_subtract_fusion.9
  798.1 4.4 convolution_subtract_fusion.8
  804.0 3.5 convolution_subtract_fusion.7
  826.2 5.1 convolution_subtract_fusion.11
  832.9 4.5 broadcast_select_fusion
  840.7 11.7 %bitcast_select_fusion = f32[256,128,128]{2,1,0:T(8,128)} fusion(f32[128,2,128,128]{3,2,1,0:T(8,128)} %all-to-all-done.2, pred[256]{0:T(512)(128)(4,1)S(1)} %ge.26), kind=kLoop, calls=%fused_computation.6 | loop fusion | flops 4194304 | bytes 33554688 | tf_op jit(solution)/shard_map/jit(_where)/select_n | solution.py:52
  852.4 202.1 %scatter_fusion.3 = f32[4608,128]{1,0:T(8,128)S(1)} fusion(f32[4608,128]{1,0:T(8,128)S(1)} %bitcast.183, s32[32768]{0:T(1024)S(1)} %select_bitcast_fusion, f32[32768,128]{1,0:T(8,128)} %bitcast.186), kind=kCustom, calls=%fused_computation.3 | custom fusion | flops 4194304 | bytes 50462720
  1057.5 16.9 %bitcast_subtract_fusion = f32[768,768]{1,0:T(8,128)} fusion(f32[96,8,6,128]{3,2,1,0:T(8,128)} %bitcast.188, f32[768,1536]{1,0:T(8,128)} %get-tuple-element.25, f32[768,1536]{1,0:T(8,128)} %all-reduce.6.cloned.1.call-done, pred[768]{0:T(1024)(128)(4,1)S(1)} %copy-done.15), kind=kOutput, calls=%fused_computation.19 | convolution fusion | flops 10872815616 | bytes 14156544 | tf_op jit(solution)/shard_map/dot_general | solution.py:77
  (198 shorter events, 140.5 us)
Async XLA Ops:
  7.2 114.1 %all-reduce.8.cloned.1.call-start = ((), (), s32[]{:S(2)}) async-start(), calls=%async_computation.6 | async-start | bytes 4718592 | tf_op jit(solution)/shard_map/psum | solution.py:11
  8.9 115.7 %copy-start = (f32[768,384]{0,1:T(8,128)}, f32[768,384]{0,1:T(8,128)S(1)}, u32[]{:S(2)}) copy-start(f32[768,384]{0,1:T(8,128)S(1)} %copy.63) | copy-start | bytes 3538948
  10.6 114.7 %copy-start.19 = (s32[128]{0:T(128)S(1)}, s32[128]{0:T(128)}, u32[]{:S(2)}) copy-start(s32[128]{0:T(128)} %param.9) | copy-start | bytes 1540
  10.6 114.9 %copy-start.16 = (s32[128]{0:T(128)S(1)}, s32[128]{0:T(128)}, u32[]{:S(2)}) copy-start(s32[128]{0:T(128)} %param.10) | copy-start | bytes 1540
  10.6 210.6 %all-gather.3.cloned.1.call-start = ((), (), s32[]{:S(2)}) async-start(), calls=%async_computation.3 | async-start | bytes 11796480 | tf_op jit(solution)/shard_map/all_gather | solution.py:61
  124.6 623.0 %all-gather.5.cloned.1.call-start = ((), (), s32[]{:S(2)}) async-start(), calls=%async_computation.4 | async-start | bytes 5898240 | tf_op jit(solution)/shard_map/all_gather | solution.py:63
  132.6 61.6 %all-to-all-start = ((s32[128,1,2]{2,1,0:T(1,128)}), s32[128,1,2]{2,1,0:T(1,128)S(1)}, u32[]{:S(2)}, u32[]{:S(2)}) async-start(s32[128,1,2]{2,1,0:T(1,128)} %copy.80), calls=%async_computation | async-start | bytes 131072 | tf_op jit(solution)/shard_map/all_to_all | solution.py:38
  141.6 6.8 copy-start.14
  194.3 17.4 %all-to-all-start.1 = ((s32[128,2,128]{2,1,0:T(2,128)}), s32[128,2,128]{2,1,0:T(2,128)S(1)}, u32[]{:S(2)}, u32[]{:S(2)}) async-start(s32[128,2,128]{2,1,0:T(2,128)} %scatter_fusion.1), calls=%async_computation.1 | async-start | bytes 262144 | tf_op jit(solution)/shard_map/all_to_all | solution.py:37
  205.8 13.9 %copy-start.18 = (s32[3]{0:T(128)S(1)}, s32[3]{0:T(128)}, u32[]{:S(2)}) copy-start(s32[3]{0:T(128)} %constant.472) | copy-start | bytes 40
  205.8 14.7 %copy-start.17 = (s32[3]{0:T(128)S(1)}, s32[3]{0:T(128)}, u32[]{:S(2)}) copy-start(s32[3]{0:T(128)} %constant.475) | copy-start | bytes 40
  211.7 629.1 %all-to-all-start.2 = ((f32[128,2,128,128]{3,2,1,0:T(8,128)}), f32[128,2,128,128]{3,2,1,0:T(8,128)}, u32[]{:S(2)}, u32[]{:S(2)}) async-start(f32[128,2,128,128]{3,2,1,0:T(8,128)} %scatter_fusion.2), calls=%async_computation.2 | async-start | bytes 33554432 | tf_op jit(solution)/shard_map/all_to_all | solution.py:36
  219.4 838.1 %all-reduce.6.cloned.1.call-start = ((), (), s32[]{:S(2)}) async-start(), calls=%async_computation.5 | async-start | bytes 9437184 | tf_op jit(solution)/shard_map/psum | solution.py:11
  747.5 6.0 copy-start.10
  770.3 8.5 copy-start.11
  792.4 4.1 copy-start.1
  807.5 14.9 %copy-start.2 = (f32[128,768]{0,1:T(8,128)S(1)}, f32[128,768]{0,1:T(8,128)}, u32[]{:S(2)}) copy-start(f32[128,768]{0,1:T(8,128)} %copy.67) | copy-start | bytes 1179652
  807.5 15.0 %copy-start.3 = (f32[128,768]{0,1:T(8,128)S(1)}, f32[128,768]{0,1:T(8,128)}, u32[]{:S(2)}) copy-start(f32[128,768]{0,1:T(8,128)} %copy.68) | copy-start | bytes 1179652
  807.5 15.0 %copy-start.4 = (f32[128,768]{0,1:T(8,128)S(1)}, f32[128,768]{0,1:T(8,128)}, u32[]{:S(2)}) copy-start(f32[128,768]{0,1:T(8,128)} %copy.69) | copy-start | bytes 1179652
  822.4 3.5 copy-start.9
  822.4 3.5 copy-start.8
  822.4 3.6 copy-start.7
  822.4 3.6 copy-start.6
  822.4 3.7 copy-start.5
  837.5 0.9 copy-start.12
  837.5 0.9 copy-start.13
  1054.5 3.0 copy-start.15
Sparse Core Ops, SparseCore 0:
  12.0 109.2 all-reduce.7
  124.7 93.2 all-gather.2
  220.3 231.0 all-gather.4
  837.6 113.8 all-reduce.5
where the time goes:
time: 1090 us; the launch traced here: 1080 us
  other arithmetic  636 us (58%)
  local copies, waits for them, and re-layouts  149 us (14%)
  matrix products  130 us (12%)
  waiting for transfers between devices  117 us (11%)
  starting transfers between devices  26 us (2%)
  between operations  22.6 us (2%)
    another operation x46, other arithmetic, body(): diagonal_factor = jnp.linalg.cholesky(diag_block)  264 us
    unnamed x5, other arithmetic  204 us
    another operation x3, other arithmetic, body(): jax.scipy.linalg.solve_triangular(diagonal_factor, full_rows.T, lower=True)  132 us
    psum x2, waiting for transfers between devices, from_root(): return lax.psum(kept, axis)  111 us
    another operation x23, matrix products, body(): jax.scipy.linalg.solve_triangular(diagonal_factor, full_rows.T, lower=True)  63.3 us
    another operation x22, matrix products, body(): diagonal_factor = jnp.linalg.cholesky(diag_block)  50.1 us
    another operation x36, local copies, waits for them, and re-layouts  43.4 us
    scatter x1, local copies, waits for them, and re-layouts, body(): send_tiles = send_tiles.at[child_owner, slot_index].set(child_tiles)  24.8 us
  transfers between devices with their start and end apart: 7, of which 2 were waited for; matrix products, arithmetic and copies ran while one was open for 82% of the time, Pallas kernels for 0%

commit v1 on v0

v1 whole, which is shorter than its diff:
```python
import jax
import jax.numpy as jnp
from jax import lax
from jax.experimental import pallas as pl
from jax.experimental.pallas import tpu as pltpu
from jax.sharding import PartitionSpec as P

PW = 1536
NB = 128
KB = PW // NB
TB = 128
MESH = pl.DeviceIdType.MESH
F32 = jnp.float32
BF16 = jnp.bfloat16
BIG = 60 << 20


def dot_nt(a, b):
    return lax.dot_general(
        a, b, (((1,), (1,)), ((), ())),
        precision=lax.Precision.HIGHEST, preferred_element_type=F32)


def dot_b(a, b):
    return lax.dot_general(a, b, (((1,), (1,)), ((), ())), preferred_element_type=F32)


def split2(v):
    hi = v.astype(BF16)
    return hi, (v - hi.astype(F32)).astype(BF16)


def dot3(ah, al, bh, bl):
    return dot_b(ah, bh) + (dot_b(ah, bl) + dot_b(al, bh))


def pack_kernel(dst_ref, tiles_ref, rows_ref, out_ref, stage, sems):
    step = pl.program_id(0)
    steps = pl.num_programs(0)
    slot = lax.rem(step, 2)
    per = tiles_ref.shape[0]

    def copy(at, i, which):
        return pltpu.make_async_copy(
            stage.at[which, i], out_ref.at[dst_ref[at * per + i]], sems.at[which, i])

    @pl.when(step >= 2)
    def _():
        for i in range(per):
            copy(step - 2, i, slot).wait()

    sub = lax.broadcasted_iota(jnp.int32, (TB, TB), 0)
    for i in range(per):
        pick = jnp.where(sub == rows_ref[i:i + 1, :], 1.0, 0.0).astype(BF16)
        tile = tiles_ref[i]
        hi = tile.astype(BF16)
        rest = tile - hi.astype(F32)
        mid = rest.astype(BF16)
        low = (rest - mid.astype(F32)).astype(BF16)
        moved = jnp.dot(pick, hi, preferred_element_type=F32)
        moved = moved + jnp.dot(pick, mid, preferred_element_type=F32)
        moved = moved + jnp.dot(pick, low, preferred_element_type=F32)
        stage[slot, i] = moved
    for i in range(per):
        copy(step, i, slot).start()

    @pl.when(step == steps - 1)
    def _():
        for i in range(per):
            copy(step - 1, i, 1 - slot).wait()
        for i in range(per):
            copy(step, i, slot).wait()


def pack(dst, tiles, rows, slots):
    count = tiles.shape[0]
    per = 8
    return pl.pallas_call(
        pack_kernel,
        grid_spec=pltpu.PrefetchScalarGridSpec(
            num_scalar_prefetch=1,
            grid=(count // per,),
            in_specs=[
                pl.BlockSpec((per, TB, TB), lambda i, d: (i, 0, 0)),
                pl.BlockSpec((per, TB), lambda i, d: (i, 0)),
            ],
            out_specs=pl.BlockSpec(memory_space=pl.ANY),
            scratch_shapes=[
                pltpu.VMEM((2, per, TB, TB), F32),
                pltpu.SemaphoreType.DMA((2, per)),
            ],
        ),
        out_shape=jax.ShapeDtypeStruct((slots, TB, TB), F32),
        name="pack",
    )(dst, tiles, rows)


def bcast_kernel(pa_ref, pc_ref, ga_ref, gc_ref,
                 s1a, s1c, r1a, r1c, loc, ss, rs, fs, fr, xs, xr):
    row = lax.axis_index("row")
    y = lax.axis_index("col")
    core = lax.rem(row, 2)
    z = lax.rem(lax.div(row, 2), 4)
    x = lax.div(row, 8)
    xz = lax.div(row, 2)
    pos = {"x": x, "y": y, "z": z}

    def device(axis, p):
        q = dict(pos)
        q[axis] = p
        return ((q["x"] * 4 + q["z"]) * 2 + core, q["y"])

    def remote(src, dst, send, recv, dev):
        return pltpu.make_async_remote_copy(
            src_ref=src, dst_ref=dst, send_sem=send, recv_sem=recv,
            device_id=dev, device_id_type=MESH)

    def piece_a(q):
        return pa_ref.at[:, q], ga_ref.at[:, y, core, lax.div(q, 4), lax.rem(q, 4)]

    def send_a(q):
        s, d = piece_a(q)
        return remote(s, d, s1a.at[q], r1a.at[0], (q * 2 + core, y))

    to_col = row - 2
    to_core = lax.div(y, 2)

    def piece_c(q):
        return pc_ref.at[q], gc_ref.at[y, lax.div(q, 4), lax.rem(q, 4)]

    def send_c(q):
        s, d = piece_c(q)
        return remote(s, d, s1c.at[q], r1c.at[lax.rem(y, 2)], (q * 2 + to_core, to_col))

    is_a = row < 2
    is_c = (row >= 2) & (row < 6)

    @pl.when(is_a)
    def _():
        s, d = piece_a(0)
        pltpu.make_async_copy(s, d, loc.at[0]).start()

        @pl.loop(1, 16)
        def _(q):
            send_a(q).start()

    def keeps(q):
        return (q == xz) & (to_core == core) & (to_col == y)

    @pl.when(is_c)
    def _():
        @pl.loop(0, 16)
        def _(q):
            @pl.when(keeps(q))
            def _():
                s, d = piece_c(q)
                pltpu.make_async_copy(s, d, loc.at[1]).start()

            @pl.when(jnp.logical_not(keeps(q)))
            def _():
                send_c(q).start()

    @pl.when(is_a)
    def _():
        s, d = piece_a(0)
        pltpu.make_async_copy(s, d, loc.at[0]).wait()

    @pl.when(jnp.logical_not(is_a))
    def _():
        s = pa_ref.at[:, 0]
        remote(s, ga_ref.at[:, y, core, x, z], s1a.at[0], r1a.at[0], (row, y)).wait_recv()

    for h in range(2):
        yy = 2 * core + h
        mine = (yy == y) & (row == y + 2)

        @pl.when(mine)
        def _():
            s, d = piece_c(xz)
            pltpu.make_async_copy(s, d, loc.at[1]).wait()

        @pl.when(jnp.logical_not(mine))
        def _():
            remote(pc_ref.at[0], gc_ref.at[yy, x, z], s1c.at[0], r1c.at[h], (row, y)).wait_recv()

    chains = []
    for s, order in enumerate((("z", "x", "y"), ("x", "y", "z"), ("y", "z", "x"))):
        chains.append(("a", s, order))
    for s, order in enumerate((("z", "x"), ("x", "z"))):
        chains.append(("c", s, order))

    def block(kind, s, order, t, p, half=None):
        ind = {}
        for j, a in enumerate(order):
            ind[a] = slice(None) if j < t else (p if j == t else pos[a])
        if kind == "a":
            tail = () if half is None else (pl.ds(8 * half, 8), slice(None))
            fill = () if half is None else tail
            return ga_ref.at[(s, ind["y"], core, ind["x"], ind["z"]) + fill]
        fill = () if half is None else (pl.ds(24 * half, 24), slice(None))
        return gc_ref.at[(2 * core + s, ind["x"], ind["z"]) + fill]

    sibling = (xz * 2 + (1 - core), y)

    def near(n, t, up):
        kind, s, order = chains[n]
        a = order[t]
        p = pos[a]
        b = block(kind, s, order, t, p)
        return remote(b, b, ss.at[n, t, up], rs.at[n, t, up],
                      device(a, lax.rem(p + (1 if up else 3), 4)))

    def near_wait(n, t, up):
        kind, s, order = chains[n]
        a = order[t]
        b = block(kind, s, order, t, lax.rem(pos[a] + (3 if up else 1), 4))
        remote(b, b, ss.at[n, t, up], rs.at[n, t, up], (row, y)).wait_recv()

    def far(n, t, up):
        kind, s, order = chains[n]
        a = order[t]
        p = pos[a]
        b = block(kind, s, order, t, lax.rem(p + (3 if up else 1), 4), 0 if up else 1)
        return remote(b, b, fs.at[n, t, up], fr.at[n, t, up],
                      device(a, lax.rem(p + (1 if up else 3), 4)))

    def far_wait(n, t, up):
        kind, s, order = chains[n]
        a = order[t]
        b = block(kind, s, order, t, lax.rem(pos[a] + 2, 4), 0 if up else 1)
        remote(b, b, fs.at[n, t, up], fr.at[n, t, up], (row, y)).wait_recv()

    def cross(n, shift):
        kind, s, order = chains[n]
        t = len(order) - 1
        b = block(kind, s, order, t, lax.rem(pos[order[t]] + shift, 4))
        return remote(b, b, xs.at[n, shift], xr.at[n, shift], sibling)

    def cross_wait(n, shift):
        kind, s, order = chains[n]
        t = len(order) - 1
        ind = {}
        for j, a in enumerate(order):
            ind[a] = slice(None) if j < t else lax.rem(pos[a] + shift, 4)
        if kind == "a":
            b = ga_ref.at[s, ind["y"], 1 - core, ind["x"], ind["z"]]
        else:
            b = gc_ref.at[2 * (1 - core) + s, ind["x"], ind["z"]]
        remote(b, b, xs.at[n, shift], xr.at[n, shift], (row, y)).wait_recv()

    for t in range(3):
        live = [n for n in range(5) if t < len(chains[n][2])]
        last = [n for n in live if t == len(chains[n][2]) - 1]
        for n in live:
            for up in range(2):
                near(n, t, up).start()
        for n in last:
            cross(n, 0).start()
        for n in live:
            for up in range(2):
                near_wait(n, t, up)
                far(n, t, up).start()
                if n in last:
                    cross(n, 3 if up else 1).start()
        for n in live:
            for up in range(2):
                far_wait(n, t, up)
        for n in last:
            cross(n, 2).start()
    for n in range(5):
        for shift in range(4):
            cross_wait(n, shift)
    for n in range(5):
        for t in range(len(chains[n][2])):
            for up in range(2):
                near(n, t, up).wait_send()
                far(n, t, up).wait_send()
        for shift in range(4):
            cross(n, shift).wait_send()

    @pl.when(is_a)
    def _():
        @pl.loop(1, 16)
        def _(q):
            send_a(q).wait_send()

    @pl.when(is_c)
    def _():
        @pl.loop(0, 16)
        def _(q):
            @pl.when(jnp.logical_not(keeps(q)))
            def _():
                send_c(q).wait_send()


def bcast(panel):
    rows, cols = panel.shape
    dma = pltpu.SemaphoreType.DMA
    return pl.pallas_call(
        bcast_kernel,
        in_specs=[pl.BlockSpec(memory_space=pl.ANY)] * 2,
        out_specs=[pl.BlockSpec(memory_space=pl.ANY)] * 2,
        out_shape=[
            jax.ShapeDtypeStruct((3, 4, 2, 4, 4, 16, cols), F32),
            jax.ShapeDtypeStruct((4, 4, 4, 48, cols), F32),
        ],
        scratch_shapes=[
            dma((16,)), dma((16,)), dma((1,)), dma((2,)), dma((2,)),
            dma((5, 3, 2)), dma((5, 3, 2)), dma((5, 3, 2)), dma((5, 3, 2)),
            dma((5, 4)), dma((5, 4)),
        ],
        compiler_params=pltpu.CompilerParams(has_side_effects=True),
        name="bcast",
    )(panel.reshape(3, 16, 16, cols), panel.reshape(16, 48, cols))


def wide(v):
    return jnp.broadcast_to(v, (8, 128))


def small_inverse(cols):
    c = [[None] * 8 for _ in range(8)]
    for j in range(8):
        for i in range(j, 8):
            c[i][j] = wide(cols[j][i:i + 1, :])
    t = [[None] * 8 for _ in range(8)]
    for j in range(8):
        r = lax.rsqrt(c[j][j])
        t[j][j] = r
        for i in range(j + 1, 8):
            c[i][j] = c[i][j] * r
        for m in range(j + 1, 8):
            for i in range(m, 8):
                c[i][m] = c[i][m] - c[i][j] * c[m][j]
        for k in range(j):
            s = c[j][k] * t[k][k]
            for m in range(k + 1, j):
                s = s + c[j][m] * t[m][k]
            t[j][k] = -(s * r)
    return t


def factor_block(d):
    row = lax.broadcasted_iota(jnp.int32, (NB, NB), 0)
    col = lax.broadcasted_iota(jnp.int32, (NB, NB), 1)
    eye = jnp.where(row == col, 1.0, 0.0).astype(F32)
    groups = NB // 8
    r = [d[8 * g:8 * g + 8, :] for g in range(groups)]
    w = [eye[8 * g:8 * g + 8, :] for g in range(groups)]
    sub = lax.broadcasted_iota(jnp.int32, (8, NB), 0)
    us, vs = [], []
    for g in range(groups):
        cols = [wide(r[g][:, 8 * g + j:8 * g + j + 1]) for j in range(8)]
        t = small_inverse(cols)
        u = v = None
        for j in range(8):
            part = jnp.zeros((8, NB), F32)
            for i in range(j, 8):
                part = jnp.where(sub == i, t[i][j], part)
            du, dv = part * r[g][j:j + 1, :], part * w[g][j:j + 1, :]
            u, v = (du, dv) if u is None else (u + du, v + dv)
        us.append(u)
        vs.append(v)
        if g + 1 < groups:
            nxt = [wide(r[g + 1][:, 8 * g + j:8 * g + j + 1]) for j in range(8)]
            ra, wa = r[g + 1], w[g + 1]
            for j in range(8):
                m = nxt[0] * t[j][0]
                for k in range(1, j + 1):
                    m = m + nxt[k] * t[j][k]
                ra = ra - m * u[j:j + 1, :]
                wa = wa - m * v[j:j + 1, :]
            r[g + 1], w[g + 1] = ra, wa
        if g + 2 < groups:
            ut = jnp.transpose(u)
            for g2 in range(g + 2, groups):
                blk = ut[8 * g2:8 * g2 + 8, :]
                ra, wa = r[g2], w[g2]
                for j in range(8):
                    m = wide(blk[:, j:j + 1])
                    ra = ra - m * u[j:j + 1, :]
                    wa = wa - m * v[j:j + 1, :]
                r[g2], w[g2] = ra, wa
    upper = jnp.concatenate(us, axis=0)
    inverse = jnp.concatenate(vs, axis=0)
    return jnp.where(col >= row, upper, 0.0), inverse


def chol_kernel(ga_ref, l_ref, w_ref, c_ref):
    def given(i, j):
        r, c = i * NB, j * NB
        a, b = r % 256, c % 384
        return ga_ref[(r % 768) // 256, c // 384, r // 768, a:a + NB, b:b + NB]

    def sym(i, j):
        return 0.5 * (given(i, j) + given(j, i).T)

    def at(i):
        return slice(i * NB, (i + 1) * NB)

    d = sym(0, 0)
    last_w = None
    for k in range(KB):
        done = slice(0, k * NB)
        below = slice((k + 1) * NB, PW)
        rest = None
        if k + 1 < KB:
            if k > 0:
                l_ref[below, at(k - 1)] = dot_nt(c_ref[below, :], last_w)
                acc = dot_nt(l_ref[below, done], l_ref[at(k), done])
                for i in range(k + 1, KB):
                    c_ref[at(i), :] = sym(i, k) - acc[at(i - k - 1), :]
                nxt = l_ref[at(k + 1), done]
                rest = sym(k + 1, k + 1) - dot_nt(nxt, nxt)
            else:
                for i in range(1, KB):
                    c_ref[at(i), :] = sym(i, 0)
                rest = sym(1, 1)
        upper, inverse = factor_block(d)
        l_ref[at(k), at(k)] = upper.T
        w_ref[at(k), :] = inverse
        if k + 1 < KB:
            l_ref[at(k), below] = jnp.zeros((NB, PW - (k + 1) * NB), F32)
            nxt = dot_nt(c_ref[at(k + 1), :], inverse)
            l_ref[at(k + 1), at(k)] = nxt
            d = rest - dot_nt(nxt, nxt)
            last_w = inverse


def chol(ga):
    return pl.pallas_call(
        chol_kernel,
        out_shape=[
            jax.ShapeDtypeStruct((PW, PW), F32),
            jax.ShapeDtypeStruct((PW, NB), F32),
        ],
        scratch_shapes=[pltpu.VMEM((PW, NB), F32)],
        compiler_params=pltpu.CompilerParams(vmem_limit_bytes=BIG),
        cost_estimate=pl.CostEstimate(
            flops=60_000_000_000, bytes_accessed=20_000_000, transcendentals=0),
        name="chol",
    )(ga)


def solve_kernel(place_ref, l_ref, w_ref, pr_ref, pc_ref, t_ref, f_ref, o_ref,
                 lh, ll, wh, wl, xh, xl, keep):
    row = place_ref[0]
    col = place_ref[1]
    rows = pr_ref.shape[1]
    wide_cols = pr_ref.shape[2]
    nb = 2 * NB

    @pl.loop(0, KB)
    def _(k):
        at = pl.ds(pl.multiple_of(k * NB, NB), NB)
        hi, lo = split2(l_ref[at, :])
        lh[at, :] = hi
        ll[at, :] = lo

    for k in range(KB // 2):
        a, b = 2 * k * NB, (2 * k + 1) * NB
        w1, w2 = w_ref[a:a + NB, :], w_ref[b:b + NB, :]
        cross = l_ref[b:b + NB, a:a + NB]
        mid = jnp.dot(cross, w1, precision=lax.Precision.HIGHEST, preferred_element_type=F32)
        low = -jnp.dot(w2, mid, precision=lax.Precision.HIGHEST, preferred_element_type=F32)
        zero = jnp.zeros((NB, NB), F32)
        hi, lo = split2(jnp.concatenate(
            [jnp.concatenate([w1, zero], axis=1), jnp.concatenate([low, w2], axis=1)], axis=0))
        wh[k] = hi
        wl[k] = lo

    for part, src in enumerate((pr_ref, pc_ref)):
        for k in range(KB // 2):
            cols = []
            for j in range(2):
                at = (2 * k + j) * NB
                cols.append(src[at // wide_cols, :, at % wide_cols:at % wide_cols + NB])
            v = jnp.concatenate(cols, axis=1)
            if k > 0:
                done = slice(0, k * nb)
                here = slice(k * nb, (k + 1) * nb)
                v = v - dot3(xh[part, :, done], xl[part, :, done], lh[here, done], ll[here, done])
            vh, vl = split2(v)
            v = dot3(vh, vl, wh[k], wl[k])
            hi, lo = split2(v)
            here = slice(k * nb, (k + 1) * nb)
            xh[part, :, here] = hi
            xl[part, :, here] = lo
            if part == 0:
                for j in range(2):
                    at = (2 * k + j) * NB
                    keep[at // wide_cols, :, at % wide_cols:at % wide_cols + NB] = (
                        v[:, j * NB:(j + 1) * NB])

    @pl.when(row >= 2)
    def _():
        f_ref[...] = keep[col]
        for i in range(rows // 256):
            at = slice(i * 256, (i + 1) * 256)
            o_ref[at, :] = t_ref[at, :] - dot3(xh[0, at, :], xl[0, at, :], xh[1], xl[1])

    @pl.when(row < 2)
    def _():
        first = pl.ds(pl.multiple_of(row * rows, NB), rows)
        f_ref[...] = l_ref[first, pl.ds(pl.multiple_of(col * wide_cols, NB), wide_cols)]
        o_ref[...] = t_ref[...]


def solve(place, factor, inverse, mine, theirs, trailing):
    n, rows, cols = mine.shape
    smem = pl.BlockSpec(memory_space=pltpu.SMEM)
    vmem = pl.BlockSpec(memory_space=pltpu.VMEM)
    return pl.pallas_call(
        solve_kernel,
        in_specs=[smem] + [vmem] * 5,
        out_specs=[vmem, vmem],
        out_shape=[
            jax.ShapeDtypeStruct((rows, cols), F32),
            jax.ShapeDtypeStruct(trailing.shape, F32),
        ],
        scratch_shapes=[
            pltpu.VMEM((PW, PW), BF16), pltpu.VMEM((PW, PW), BF16),
            pltpu.VMEM((KB // 2, 2 * NB, 2 * NB), BF16), pltpu.VMEM((KB // 2, 2 * NB, 2 * NB), BF16),
            pltpu.VMEM((2, rows, PW), BF16), pltpu.VMEM((2, rows, PW), BF16),
            pltpu.VMEM((n, rows, cols), F32),
        ],
        compiler_params=pltpu.CompilerParams(vmem_limit_bytes=BIG),
        cost_estimate=pl.CostEstimate(
            flops=30_000_000_000, bytes_accessed=30_000_000, transcendentals=0),
        name="solve",
    )(place, factor, inverse, mine, theirs, trailing)


def add_kernel(target_ref, tiles_ref, base_ref, out_ref):
    step = pl.program_id(0)
    per = tiles_ref.shape[0]
    tile_cols = out_ref.shape[1] // TB

    @pl.when(step == 0)
    def _():
        out_ref[...] = base_ref[...]

    for i in range(per):
        target = target_ref[step * per + i]

        @pl.when(target >= 0)
        def _():
            r = pl.ds(pl.multiple_of(lax.div(target, tile_cols) * TB, TB), TB)
            c = pl.ds(pl.multiple_of(lax.rem(target, tile_cols) * TB, TB), TB)
            out_ref[r, c] = out_ref[r, c] + tiles_ref[i]


def extend_add(target, tiles, base):
    per = 16
    return pl.pallas_call(
        add_kernel,
        grid_spec=pltpu.PrefetchScalarGridSpec(
            num_scalar_prefetch=1,
            grid=(tiles.shape[0] // per,),
            in_specs=[
                pl.BlockSpec((per, TB, TB), lambda i, t: (i, 0, 0)),
                pl.BlockSpec(base.shape, lambda i, t: (0, 0)),
            ],
            out_specs=pl.BlockSpec(base.shape, lambda i, t: (0, 0)),
        ),
        out_shape=jax.ShapeDtypeStruct(base.shape, F32),
        compiler_params=pltpu.CompilerParams(vmem_limit_bytes=32 << 20),
        name="extend_add",
    )(target, tiles, base)


def body(panel, trailing, child_tiles, child_owner, child_tile, child_rows):
    devices = lax.axis_size("row") * lax.axis_size("col")
    count = child_owner.shape[0]
    cap = 2
    both = ("row", "col")
    order = jnp.arange(count, dtype=jnp.int32)
    same = child_owner[:, None] == child_owner[None, :]
    rank = jnp.sum(jnp.where(same & (order[None, :] < order[:, None]), 1, 0), axis=1)
    dst = (child_owner * cap + rank).astype(jnp.int32)
    slots = devices * cap
    hit = dst[:, None] == jnp.arange(slots, dtype=jnp.int32)[None, :]
    target = (jnp.sum(jnp.where(hit, child_tile[:, None] + 1, 0), axis=0) - 1).astype(jnp.int32)
    got_target = lax.all_to_all(
        target.reshape(devices, cap), both, split_axis=0, concat_axis=0, tiled=True)
    packed = pack(dst, child_tiles, child_rows, slots)
    got = lax.all_to_all(
        packed.reshape(devices, cap, TB, TB), both, split_axis=0, concat_axis=0, tiled=True)

    mine = lax.all_gather(panel, "col", axis=0)
    ga, gc = bcast(panel)
    factor, inverse = chol(ga.reshape(3, 4, 2, 256, panel.shape[1]))
    place = jnp.stack([lax.axis_index("row"), lax.axis_index("col")]).astype(jnp.int32)
    factor_panel, base = solve(
        place, factor, inverse, mine, gc.reshape(4, panel.shape[0], panel.shape[1]), trailing)
    new_trailing = extend_add(got_target.reshape(-1), got.reshape(-1, TB, TB), base)
    return factor_panel, new_trailing


def solution(mesh):
    in_specs = (
        P("row", "col"),
        P("row", "col"),
        P(("row", "col"), None, None),
        P(("row", "col")),
        P(("row", "col")),
        P(("row", "col"), None),
    )
    out_specs = (P("row", "col"), P("row", "col"))
    return jax.shard_map(body, mesh=mesh, in_specs=in_specs, out_specs=out_specs, check_vma=False)
```

time: 1090 us -> 487 us (0.45)
  other arithmetic: 636 us -> 3.16 us
  Pallas kernels: 0 us -> 439 us
  local copies, waits for them, and re-layouts: 149 us -> 3.09 us
  matrix products: 130 us -> 0 us
  waiting for transfers between devices: 117 us -> 0.71 us
    pallas_call x0 -> x5, Pallas kernels: none -> 439 us  [the longest x1 292 us: bcast(): pl.pallas_call(bcast_kernel, in_specs=[pl.BlockSpec(memory_space=pl.ANY)]...]
    another operation x49 -> x1, other arithmetic: 396 us -> 0.65 us  [body(): jnp.stack([lax.axis_index('row'), lax.axis_index('col')]).astype(jnp.int32)]
    unnamed x5 -> x0, other arithmetic: 204 us -> none
    another operation x45 -> x0, matrix products: 113 us -> none  [the longest x23 63.3 us: body(): jax.scipy.linalg.solve_triangular(diagonal_factor, full_rows.T, lower=True)]
    psum x2 -> x0, waiting for transfers between devices: 111 us -> none  [from_root(): return lax.psum(kept, axis)]
    another operation x60 -> x0, local copies, waits for them, and re-layouts: 67.3 us -> none
    scatter x3 -> x0, local copies, waits for them, and re-layouts: 44.4 us -> none  [the longest x1 24.8 us: body(): send_tiles = send_tiles.at[child_owner, slot_index].set(child_tiles)]
    select_n x5 -> x0, other arithmetic: 17.9 us -> none  [the longest x1 11.7 us: body(): jnp.where(is_valid[:, None, None], got_tiles, 0.0)]
  transfers between devices with their start and end apart: 7 -> 3, of which waited for: 2 -> 0; matrix products, arithmetic and copies ran while one was open for 82% -> 0% of each run, Pallas kernels for 0% -> 88%
where the time goes in v1:
time: 487 us; the launch traced here: 481 us
  Pallas kernels  439 us (90%)
  starting transfers between devices  20.6 us (4%)
  between operations  14.6 us (3%)
    pallas_call x1, Pallas kernels, bcast(): pl.pallas_call(bcast_kernel, in_specs=[pl.BlockSpec(memory_space=pl.ANY)]...  292 us
    pallas_call x1, Pallas kernels, chol(): pl.pallas_call(chol_kernel, out_shape=[jax.ShapeDtypeStruct((PW, PW), F32...  75.3 us
    pallas_call x1, Pallas kernels, solve(): pl.pallas_call(solve_kernel, in_specs=[smem] + [vmem] * 5, out_specs=[vme...  42 us
    pallas_call x1, Pallas kernels, pack(): pl.pallas_call(pack_kernel, grid_spec=pltpu.PrefetchScalarGridSpec(num_sc...  15.1 us
    pallas_call x1, Pallas kernels, extend_add(): pl.pallas_call(add_kernel, grid_spec=pltpu.PrefetchScalarGridSpec(num_sca...  14.4 us
    all_to_all x1, starting transfers between devices, body(): lax.all_to_all(packed.reshape(devices, cap, TB, TB), both, split_axis=0,...  10.3 us
    all_to_all x1, starting transfers between devices, body(): lax.all_to_all(target.reshape(devices, cap), both, split_axis=0, concat_a...  10.3 us
  transfers between devices with their start and end apart: 3, of which 0 were waited for; matrix products, arithmetic and copies ran while one was open for 0% of the time, Pallas kernels for 88%

profile of v1, /device:TPU:26, one launch (start us, length us, event | category | flops | bytes accessed | tf_op | source)
XLA Modules:
  0.0 480.9 jit_solution(12213568443898402681)
XLA Ops:
  7.2 0.9 select_reduce_fusion.1
  8.1 0.7 multiply_add_fusion
  8.8 0.0 copy-start.1
  8.8 0.1 select_reduce_fusion
  8.9 0.8 sub.7
  9.6 10.3 %all-to-all-start = ((s32[128,1,2]{2,1,0:T(1,128)}), s32[128,1,2]{2,1,0:T(1,128)S(1)}, u32[]{:S(2)}, u32[]{:S(2)}) async-start(s32[128,1,2]{2,1,0:T(1,128)} %bitcast.7), calls=%async_computation | async-start | bytes 131072 | tf_op jit(solution)/shard_map/all_to_all | solution.py:584
  19.9 0.0 copy-done.1
  19.9 15.1 %pack.1 = f32[256,128,128]{2,1,0:T(8,128)} custom-call(s32[128]{0:T(128)} %copy-done.1, f32[128,128,128]{2,1,0:T(8,128)} %tiles_ref.1, s32[128,128]{1,0:T(8,128)} %rows_ref.1), custom_call_target="tpu_custom_call" | custom-call | tf_op jit(solution)/shard_map/pack/pallas_call | solution.py:78
  35.0 0.0 all-to-all-done
  35.0 10.3 %all-to-all-start.1 = ((f32[128,2,128,128]{3,2,1,0:T(8,128)}), f32[128,2,128,128]{3,2,1,0:T(8,128)}, u32[]{:S(2)}, u32[]{:S(2)}) async-start(f32[128,2,128,128]{3,2,1,0:T(8,128)} %bitcast.10), calls=%async_computation.1 | async-start | bytes 33554432 | tf_op jit(solution)/shard_map/all_to_all | solution.py:587
  45.3 0.0 all-gather.3.cloned.1.call-start
  45.3 0.7 all-gather.3.cloned.1.call-update
  46.0 292.0 %bcast.1 = (f32[3,4,2,4,4,16,384]{6,5,4,3,2,1,0:T(8,128)}, f32[4,4,4,48,384]{4,3,2,1,0:T(8,128)}) custom-call(f32[3,16,16,384]{3,2,1,0:T(8,128)} %bitcast.11, f32[16,48,384]{2,1,0:T(8,128)} %bitcast.12), custom_call_target="tpu_custom_call" | custom-call | tf_op jit(solution)/shard_map/bcast/pallas_call | solution.py:299
  338.1 0.7 pad_add_fusion.place_ref
  338.7 75.3 %chol.1 = (f32[1536,1536]{1,0:T(8,128)}, f32[1536,128]{1,0:T(8,128)}) custom-call(f32[3,4,2,256,384]{4,3,2,1,0:T(8,128)} %bitcast.13), custom_call_target="tpu_custom_call" | custom-call | flops 60000002048 | bytes 20000000 | tf_op jit(solution)/shard_map/chol/pallas_call | solution.py:431
  414.0 0.5 broadcast.23
  414.6 0.8 reduce.3
  415.4 0.1 reshape.51.target_ref
  415.5 0.0 all-gather.3.cloned.1.call-done
  415.5 42.0 %solve.1 = (f32[768,384]{1,0:T(8,128)}, f32[768,768]{1,0:T(8,128)}) custom-call(s32[2]{0:T(128)} %pad_add_fusion.place_ref, f32[1536,1536]{1,0:T(8,128)} %get-tuple-element.9.l_ref, f32[1536,128]{1,0:T(8,128)} %get-tuple-element.10.w_ref, f32[4,768,384]{2,1,0:T(8,128)} %bitcast.14, f32[4,768,384]{2,1,0:T(8,128)} %bitcast.15, f32[768,768]{1,0:T(8,128)} %t_ref.1), custom_call_target="tpu_custom_call" | custom-call | flops 30000001024 | bytes 30000000 | tf_op jit(solution)/shard_map/solve/pallas_call | solution.py:513
  457.5 0.0 all-to-all-done.1
  457.5 0.0 copy-start
  457.6 1.7 copy-done
  459.2 14.4 %extend_add.1 = f32[768,768]{1,0:T(8,128)} custom-call(s32[256]{0:T(256)S(1)} %reshape.51.target_ref, f32[256,128,128]{2,1,0:T(8,128)} %bitcast.9.tiles_ref, f32[768,768]{1,0:T(8,128)S(1)} %copy-done), custom_call_target="tpu_custom_call" | custom-call | tf_op jit(solution)/shard_map/extend_add/pallas_call | solution.py:555
  (1 shorter events, 0.0 us)
Async XLA Ops:
  8.8 11.2 %copy-start.1 = (s32[128]{0:T(128)}, s32[128]{0:T(128)S(1)}, u32[]{:S(2)}) copy-start(s32[128]{0:T(128)S(1)} %get-tuple-element.14.dst_ref) | copy-start | bytes 1540
  9.6 25.4 %all-to-all-start = ((s32[128,1,2]{2,1,0:T(1,128)}), s32[128,1,2]{2,1,0:T(1,128)S(1)}, u32[]{:S(2)}, u32[]{:S(2)}) async-start(s32[128,1,2]{2,1,0:T(1,128)} %bitcast.7), calls=%async_computation | async-start | bytes 131072 | tf_op jit(solution)/shard_map/all_to_all | solution.py:584
  35.0 422.5 %all-to-all-start.1 = ((f32[128,2,128,128]{3,2,1,0:T(8,128)}), f32[128,2,128,128]{3,2,1,0:T(8,128)}, u32[]{:S(2)}, u32[]{:S(2)}) async-start(f32[128,2,128,128]{3,2,1,0:T(8,128)} %bitcast.10), calls=%async_computation.1 | async-start | bytes 33554432 | tf_op jit(solution)/shard_map/all_to_all | solution.py:587
  45.3 370.2 %all-gather.3.cloned.1.call-start = ((), (), s32[]{:S(2)}) async-start(), calls=%async_computation.2 | async-start | bytes 5898240 | tf_op jit(solution)/shard_map/all_gather | solution.py:590
  457.5 1.7 copy-start
Sparse Core Ops, SparseCore 0:
  47.8 237.5 all-gather.2

commit v2 on v1

--- a/solution.py
+++ b/solution.py
@@ -95,7 +95,7 @@
     )(dst, tiles, rows)
 
 
-def bcast_kernel(pa_ref, pc_ref, ga_ref, gc_ref,
+def bcast_kernel(pa_ref, pc_ref, ga_ref, gc_ref, gr_ref,
                  s1a, s1c, r1a, r1c, loc, ss, rs, fs, fr, xs, xr):
     row = lax.axis_index("row")
     y = lax.axis_index("col")
@@ -132,8 +132,53 @@
         s, d = piece_c(q)
         return remote(s, d, s1c.at[q], r1c.at[lax.rem(y, 2)], (q * 2 + to_core, to_col))
 
+    barrier = pltpu.get_barrier_semaphore()
+
+    def greet(dev):
+        pl.semaphore_signal(barrier, inc=1, device_id=dev, device_id_type=MESH)
+
+    for axis in "xyz":
+        for shift in (1, 3):
+            greet(device(axis, lax.rem(pos[axis] + shift, 4)))
+    greet((xz * 2 + (1 - core), y))
+
     is_a = row < 2
     is_c = (row >= 2) & (row < 6)
+
+    def keeps(q):
+        return (q == xz) & (to_core == core) & (to_col == y)
+
+    def mine(h):
+        return (2 * core + h == y) & (row == y + 2)
+
+    @pl.when(is_a)
+    def _():
+        @pl.loop(1, 16)
+        def _(q):
+            greet((q * 2 + core, y))
+
+    @pl.when(jnp.logical_not(is_a))
+    def _():
+        greet((core, y))
+
+    @pl.when(is_c)
+    def _():
+        @pl.loop(0, 16)
+        def _(q):
+            @pl.when(jnp.logical_not(keeps(q)))
+            def _():
+                greet((q * 2 + to_core, to_col))
+
+    for h in range(2):
+        @pl.when(jnp.logical_not(mine(h)))
+        def _():
+            greet((y + 2, 2 * core + h))
+
+    peers = 7 + jnp.where(is_a, 15, 1)
+    peers = peers + jnp.where(is_c, jnp.where((to_core == core) & (to_col == y), 15, 16), 0)
+    for h in range(2):
+        peers = peers + jnp.where(mine(h), 0, 1)
+    pl.semaphore_wait(barrier, peers)
 
     @pl.when(is_a)
     def _():
@@ -143,9 +188,6 @@
         @pl.loop(1, 16)
         def _(q):
             send_a(q).start()
-
-    def keeps(q):
-        return (q == xz) & (to_core == core) & (to_col == y)
 
     @pl.when(is_c)
     def _():
@@ -160,34 +202,13 @@
             def _():
                 send_c(q).start()
 
-    @pl.when(is_a)
-    def _():
-        s, d = piece_a(0)
-        pltpu.make_async_copy(s, d, loc.at[0]).wait()
-
-    @pl.when(jnp.logical_not(is_a))
-    def _():
-        s = pa_ref.at[:, 0]
-        remote(s, ga_ref.at[:, y, core, x, z], s1a.at[0], r1a.at[0], (row, y)).wait_recv()
-
-    for h in range(2):
-        yy = 2 * core + h
-        mine = (yy == y) & (row == y + 2)
-
-        @pl.when(mine)
-        def _():
-            s, d = piece_c(xz)
-            pltpu.make_async_copy(s, d, loc.at[1]).wait()
-
-        @pl.when(jnp.logical_not(mine))
-        def _():
-            remote(pc_ref.at[0], gc_ref.at[yy, x, z], s1c.at[0], r1c.at[h], (row, y)).wait_recv()
-
     chains = []
     for s, order in enumerate((("z", "x", "y"), ("x", "y", "z"), ("y", "z", "x"))):
         chains.append(("a", s, order))
     for s, order in enumerate((("z", "x"), ("x", "z"))):
         chains.append(("c", s, order))
+    chains.append(("r", 0, ("y",)))
+    total = len(chains)
 
     def block(kind, s, order, t, p, half=None):
         ind = {}
@@ -197,6 +218,8 @@
             tail = () if half is None else (pl.ds(8 * half, 8), slice(None))
             fill = () if half is None else tail
             return ga_ref.at[(s, ind["y"], core, ind["x"], ind["z"]) + fill]
+        if kind == "r":
+            return gr_ref.at[p] if half is None else gr_ref.at[p, pl.ds(8 * half, 8)]
         fill = () if half is None else (pl.ds(24 * half, 24), slice(None))
         return gc_ref.at[(2 * core + s, ind["x"], ind["z"]) + fill]
 
@@ -207,7 +230,8 @@
         a = order[t]
         p = pos[a]
         b = block(kind, s, order, t, p)
-        return remote(b, b, ss.at[n, t, up], rs.at[n, t, up],
+        src = pc_ref if kind == "r" else b
+        return remote(src, b, ss.at[n, t, up], rs.at[n, t, up],
                       device(a, lax.rem(p + (1 if up else 3), 4)))
 
     def near_wait(n, t, up):
@@ -248,33 +272,83 @@
             b = gc_ref.at[2 * (1 - core) + s, ind["x"], ind["z"]]
         remote(b, b, xs.at[n, shift], xr.at[n, shift], (row, y)).wait_recv()
 
-    for t in range(3):
-        live = [n for n in range(5) if t < len(chains[n][2])]
-        last = [n for n in live if t == len(chains[n][2]) - 1]
-        for n in live:
+    diag, column, own = (0, 1, 2), (3, 4), (5,)
+    for up in range(2):
+        near(5, 0, up).start()
+    @pl.when(is_a)
+    def _():
+        s, d = piece_a(0)
+        pltpu.make_async_copy(s, d, loc.at[0]).wait()
+
+    @pl.when(jnp.logical_not(is_a))
+    def _():
+        s = pa_ref.at[:, 0]
+        remote(s, ga_ref.at[:, y, core, x, z], s1a.at[0], r1a.at[0], (row, y)).wait_recv()
+
+    def begin(ns, t):
+        for n in ns:
             for up in range(2):
                 near(n, t, up).start()
-        for n in last:
-            cross(n, 0).start()
-        for n in live:
+
+    def forward(ns, t):
+        for n in ns:
             for up in range(2):
                 near_wait(n, t, up)
                 far(n, t, up).start()
-                if n in last:
+                if n < 5 and t == len(chains[n][2]) - 1:
                     cross(n, 3 if up else 1).start()
-        for n in live:
-            for up in range(2):
-                far_wait(n, t, up)
-        for n in last:
+
+    def settle(n, t):
+        for up in range(2):
+            far_wait(n, t, up)
+
+    def advance(ns, t):
+        for n in ns:
+            settle(n, t)
+            begin([n], t + 1)
+            if t + 1 == len(chains[n][2]) - 1:
+                cross(n, 0).start()
+
+    def finish(ns, t):
+        for n in ns:
+            settle(n, t)
             cross(n, 2).start()
+
+    begin(diag, 0)
+    for h in range(2):
+        yy = 2 * core + h
+
+        @pl.when(mine(h))
+        def _():
+            s, d = piece_c(xz)
+            pltpu.make_async_copy(s, d, loc.at[1]).wait()
+
+        @pl.when(jnp.logical_not(mine(h)))
+        def _():
+            remote(pc_ref.at[0], gc_ref.at[yy, x, z], s1c.at[0], r1c.at[h], (row, y)).wait_recv()
+
+    begin(column, 0)
+    forward(diag, 0)
+    forward(column, 0)
+    advance(diag, 0)
+    advance(column, 0)
+    forward(diag, 1)
+    forward(column, 1)
+    advance(diag, 1)
+    finish(column, 1)
+    forward(own, 0)
+    forward(diag, 2)
+    finish(diag, 2)
+    settle(5, 0)
     for n in range(5):
         for shift in range(4):
             cross_wait(n, shift)
-    for n in range(5):
+    for n in range(total):
         for t in range(len(chains[n][2])):
             for up in range(2):
                 near(n, t, up).wait_send()
                 far(n, t, up).wait_send()
+    for n in range(5):
         for shift in range(4):
             cross(n, shift).wait_send()
 
@@ -299,17 +373,18 @@
     return pl.pallas_call(
         bcast_kernel,
         in_specs=[pl.BlockSpec(memory_space=pl.ANY)] * 2,
-        out_specs=[pl.BlockSpec(memory_space=pl.ANY)] * 2,
+        out_specs=[pl.BlockSpec(memory_space=pl.ANY)] * 3,
         out_shape=[
             jax.ShapeDtypeStruct((3, 4, 2, 4, 4, 16, cols), F32),
             jax.ShapeDtypeStruct((4, 4, 4, 48, cols), F32),
+            jax.ShapeDtypeStruct((4, 16, 48, cols), F32),
         ],
         scratch_shapes=[
             dma((16,)), dma((16,)), dma((1,)), dma((2,)), dma((2,)),
-            dma((5, 3, 2)), dma((5, 3, 2)), dma((5, 3, 2)), dma((5, 3, 2)),
+            dma((6, 3, 2)), dma((6, 3, 2)), dma((6, 3, 2)), dma((6, 3, 2)),
             dma((5, 4)), dma((5, 4)),
         ],
-        compiler_params=pltpu.CompilerParams(has_side_effects=True),
+        compiler_params=pltpu.CompilerParams(has_side_effects=True, collective_id=0),
         name="bcast",
     )(panel.reshape(3, 16, 16, cols), panel.reshape(16, 48, cols))
 
@@ -387,44 +462,49 @@
 
 
 def chol_kernel(ga_ref, l_ref, w_ref, c_ref):
+    def at(i):
+        if isinstance(i, int):
+            return slice(i * NB, (i + 1) * NB)
+        return pl.ds(pl.multiple_of(i * NB, NB), NB)
+
     def given(i, j):
-        r, c = i * NB, j * NB
-        a, b = r % 256, c % 384
-        return ga_ref[(r % 768) // 256, c // 384, r // 768, a:a + NB, b:b + NB]
+        r, q = lax.rem(i, 6), lax.rem(i, 2)
+        return ga_ref[lax.div(r, 2), lax.div(j, 3), lax.div(i, 6), at(q), at(lax.rem(j, 3))]
 
     def sym(i, j):
         return 0.5 * (given(i, j) + given(j, i).T)
 
-    def at(i):
-        return slice(i * NB, (i + 1) * NB)
-
-    d = sym(0, 0)
-    last_w = None
-    for k in range(KB):
-        done = slice(0, k * NB)
-        below = slice((k + 1) * NB, PW)
-        rest = None
-        if k + 1 < KB:
-            if k > 0:
-                l_ref[below, at(k - 1)] = dot_nt(c_ref[below, :], last_w)
-                acc = dot_nt(l_ref[below, done], l_ref[at(k), done])
-                for i in range(k + 1, KB):
-                    c_ref[at(i), :] = sym(i, k) - acc[at(i - k - 1), :]
-                nxt = l_ref[at(k + 1), done]
-                rest = sym(k + 1, k + 1) - dot_nt(nxt, nxt)
-            else:
-                for i in range(1, KB):
-                    c_ref[at(i), :] = sym(i, 0)
-                rest = sym(1, 1)
-        upper, inverse = factor_block(d)
-        l_ref[at(k), at(k)] = upper.T
-        w_ref[at(k), :] = inverse
-        if k + 1 < KB:
-            l_ref[at(k), below] = jnp.zeros((NB, PW - (k + 1) * NB), F32)
-            nxt = dot_nt(c_ref[at(k + 1), :], inverse)
-            l_ref[at(k + 1), at(k)] = nxt
-            d = rest - dot_nt(nxt, nxt)
-            last_w = inverse
+    l_ref[...] = jnp.zeros_like(l_ref)
+    w_ref[...] = jnp.zeros_like(w_ref)
+    c_ref[...] = jnp.zeros_like(c_ref)
+    d = sym(jnp.int32(0), jnp.int32(0))
+    per = 4
+    for stage in range(KB // per):
+        top = stage * per
+        below = slice(top * NB, PW)
+        known = slice(0, (top + per) * NB)
+        index = top * NB + lax.broadcasted_iota(jnp.int32, (PW - top * NB, NB), 0)
+
+        def step(k, d):
+            last = jnp.maximum(k - 1, 0)
+            after = jnp.minimum(k + 1, KB - 1)
+            column = dot_nt(c_ref[below, :], w_ref[at(last), :])
+            fresh = (index >= k * NB) & (k > 0)
+            l_ref[below, at(last)] = jnp.where(fresh, column, l_ref[below, at(last)])
+            acc = dot_nt(l_ref[below, known], l_ref[at(k), known])
+            for i in range(top, KB):
+                c_ref[at(i), :] = sym(jnp.int32(i), k) - acc[at(i - top), :]
+            row = l_ref[at(after), known]
+            rest = sym(after, after) - dot_nt(row, row)
+
+            upper, inverse = factor_block(d)
+            w_ref[at(k), :] = inverse
+            nxt = dot_nt(c_ref[at(after), :], inverse)
+            l_ref[at(after), at(k)] = nxt
+            l_ref[at(k), at(k)] = upper.T
+            return rest - dot_nt(nxt, nxt)
+
+        d = lax.fori_loop(top, top + per, step, d)
 
 
 def chol(ga):
@@ -442,7 +522,7 @@
     )(ga)
 
 
-def solve_kernel(place_ref, l_ref, w_ref, pr_ref, pc_ref, t_ref, f_ref, o_ref,
+def solve_kernel(place_ref, l_ref, w_ref, own_ref, pr_ref, pc_ref, t_ref, f_ref, o_ref,
                  lh, ll, wh, wl, xh, xl, keep):
     row = place_ref[0]
     col = place_ref[1]
@@ -469,34 +549,44 @@
         wh[k] = hi
         wl[k] = lo
 
+    half = rows // 2
     for part, src in enumerate((pr_ref, pc_ref)):
-        for k in range(KB // 2):
-            cols = []
-            for j in range(2):
-                at = (2 * k + j) * NB
-                cols.append(src[at // wide_cols, :, at % wide_cols:at % wide_cols + NB])
-            v = jnp.concatenate(cols, axis=1)
-            if k > 0:
-                done = slice(0, k * nb)
+        @pl.loop(0, 2)
+        def _(g):
+            band = pl.ds(pl.multiple_of(g * half, NB), half)
+            for k in range(KB // 2):
+                cols = []
+                for h in range(2):
+                    at = (2 * k + h) * NB
+                    j, cut = at // wide_cols, slice(at % wide_cols, at % wide_cols + NB)
+                    piece = src[j, band, cut]
+                    if part == 0:
+                        piece = jnp.where(col == j, own_ref[band, cut], piece)
+                    cols.append(piece)
+                v = jnp.concatenate(cols, axis=1)
                 here = slice(k * nb, (k + 1) * nb)
-                v = v - dot3(xh[part, :, done], xl[part, :, done], lh[here, done], ll[here, done])
-            vh, vl = split2(v)
-            v = dot3(vh, vl, wh[k], wl[k])
-            hi, lo = split2(v)
-            here = slice(k * nb, (k + 1) * nb)
-            xh[part, :, here] = hi
-            xl[part, :, here] = lo
-            if part == 0:
-                for j in range(2):
-                    at = (2 * k + j) * NB
-                    keep[at // wide_cols, :, at % wide_cols:at % wide_cols + NB] = (
-                        v[:, j * NB:(j + 1) * NB])
+                if k > 0:
+                    done = slice(0, k * nb)
+                    v = v - dot3(xh[part, band, done], xl[part, band, done],
+                                 lh[here, done], ll[here, done])
+                vh, vl = split2(v)
+                v = dot3(vh, vl, wh[k], wl[k])
+                hi, lo = split2(v)
+                xh[part, band, here] = hi
+                xl[part, band, here] = lo
+                if part == 0:
+                    for h in range(2):
+                        at = (2 * k + h) * NB
+                        keep[at // wide_cols, band, at % wide_cols:at % wide_cols + NB] = (
+                            v[:, h * NB:(h + 1) * NB])
 
     @pl.when(row >= 2)
     def _():
         f_ref[...] = keep[col]
-        for i in range(rows // 256):
-            at = slice(i * 256, (i + 1) * 256)
+
+        @pl.loop(0, rows // 256)
+        def _(i):
+            at = pl.ds(pl.multiple_of(i * 256, 256), 256)
             o_ref[at, :] = t_ref[at, :] - dot3(xh[0, at, :], xl[0, at, :], xh[1], xl[1])
 
     @pl.when(row < 2)
@@ -506,13 +596,13 @@
         o_ref[...] = t_ref[...]
 
 
-def solve(place, factor, inverse, mine, theirs, trailing):
+def solve(place, factor, inverse, own, mine, theirs, trailing):
     n, rows, cols = mine.shape
     smem = pl.BlockSpec(memory_space=pltpu.SMEM)
     vmem = pl.BlockSpec(memory_space=pltpu.VMEM)
     return pl.pallas_call(
         solve_kernel,
-        in_specs=[smem] + [vmem] * 5,
+        in_specs=[smem] + [vmem] * 6,
         out_specs=[vmem, vmem],
         out_shape=[
             jax.ShapeDtypeStruct((rows, cols), F32),
@@ -528,7 +618,7 @@
         cost_estimate=pl.CostEstimate(
             flops=30_000_000_000, bytes_accessed=30_000_000, transcendentals=0),
         name="solve",
-    )(place, factor, inverse, mine, theirs, trailing)
+    )(place, factor, inverse, own, mine, theirs, trailing)
 
 
 def add_kernel(target_ref, tiles_ref, base_ref, out_ref):
@@ -584,15 +674,15 @@
     got_target = lax.all_to_all(
         target.reshape(devices, cap), both, split_axis=0, concat_axis=0, tiled=True)
     packed = pack(dst, child_tiles, child_rows, slots)
+    ga, gc, mine = bcast(panel)
+    packed, ga = lax.optimization_barrier((packed, ga))
     got = lax.all_to_all(
         packed.reshape(devices, cap, TB, TB), both, split_axis=0, concat_axis=0, tiled=True)
-
-    mine = lax.all_gather(panel, "col", axis=0)
-    ga, gc = bcast(panel)
+    row_index, col_index = lax.axis_index("row"), lax.axis_index("col")
     factor, inverse = chol(ga.reshape(3, 4, 2, 256, panel.shape[1]))
-    place = jnp.stack([lax.axis_index("row"), lax.axis_index("col")]).astype(jnp.int32)
+    place = jnp.stack([row_index, col_index]).astype(jnp.int32)
     factor_panel, base = solve(
-        place, factor, inverse, mine, gc.reshape(4, panel.shape[0], panel.shape[1]), trailing)
+        place, factor, inverse, panel, mine.reshape(4, *panel.shape), gc.reshape(4, *panel.shape), trailing)
     new_trailing = extend_add(got_target.reshape(-1), got.reshape(-1, TB, TB), base)
     return factor_panel, new_trailing
 

time: 487 us -> 375 us (0.77); the launches traced: 481 us -> 375 us
  Pallas kernels: 439 us -> 250 us
  waiting for transfers between devices: 0.71 us -> 95 us
  between operations: 14.6 us -> 0.71 us
    pallas_call x1, Pallas kernels: 292 us -> 82.6 us  [bcast(): pl.pallas_call(bcast_kernel, in_specs=[pl.BlockSpec(memory_space=pl.ANY)]...]
    all_to_all x1, waiting for transfers between devices: 0.01 us -> 95 us  [body(): lax.all_to_all(packed.reshape(devices, cap, TB, TB), both, split_axis=0,...]
    pallas_call x1, Pallas kernels: 75.3 us -> 93 us  [chol(): pl.pallas_call(chol_kernel, out_shape=[jax.ShapeDtypeStruct((PW, PW), F32...]
  transfers between devices with their start and end apart: 3 -> 2, of which waited for: 0 -> 1; matrix products, arithmetic and copies ran while one was open for 0% -> 1% of each run, Pallas kernels for 88% -> 63%
where the time goes in v2:
time: 375 us
  Pallas kernels  250 us (67%)
  waiting for transfers between devices  95 us (25%)
  starting transfers between devices  22.4 us (6%)
    all_to_all x1, waiting for transfers between devices, body(): lax.all_to_all(packed.reshape(devices, cap, TB, TB), both, split_axis=0,...  95 us
    pallas_call x1, Pallas kernels, chol(): pl.pallas_call(chol_kernel, out_shape=[jax.ShapeDtypeStruct((PW, PW), F32...  93 us
    pallas_call x1, Pallas kernels, bcast(): pl.pallas_call(bcast_kernel, in_specs=[pl.BlockSpec(memory_space=pl.ANY)]...  82.6 us
    pallas_call x1, Pallas kernels, solve(): pl.pallas_call(solve_kernel, in_specs=[smem] + [vmem] * 6, out_specs=[vme...  44.8 us
    pallas_call x1, Pallas kernels, pack(): pl.pallas_call(pack_kernel, grid_spec=pltpu.PrefetchScalarGridSpec(num_sc...  15.2 us
    pallas_call x1, Pallas kernels, extend_add(): pl.pallas_call(add_kernel, grid_spec=pltpu.PrefetchScalarGridSpec(num_sca...  14.5 us
    all_to_all x1, starting transfers between devices, body(): lax.all_to_all(packed.reshape(devices, cap, TB, TB), both, split_axis=0,...  12.1 us
    all_to_all x1, starting transfers between devices, body(): lax.all_to_all(target.reshape(devices, cap), both, split_axis=0, concat_a...  10.3 us
  transfers between devices with their start and end apart: 2, of which 1 were waited for; matrix products, arithmetic and copies ran while one was open for 1% of the time, Pallas kernels for 63%

profile of v2, /device:TPU:26, one launch (start us, length us, event | category | flops | bytes accessed | tf_op | source)
XLA Modules:
  0.0 374.5 jit_solution(3273656601040772398)
XLA Ops:
  0.6 0.9 select_reduce_fusion.1
  1.5 0.7 multiply_add_fusion
  2.2 0.0 copy-start.1
  2.2 0.1 select_reduce_fusion
  2.3 0.8 sub.7
  3.1 10.3 %all-to-all-start = ((s32[128,1,2]{2,1,0:T(1,128)}), s32[128,1,2]{2,1,0:T(1,128)S(1)}, u32[]{:S(2)}, u32[]{:S(2)}) async-start(s32[128,1,2]{2,1,0:T(1,128)} %bitcast.7), calls=%async_computation | async-start | bytes 131072 | tf_op jit(solution)/shard_map/all_to_all | solution.py:674
  13.4 82.6 %bcast.1 = (f32[3,4,2,4,4,16,384]{6,5,4,3,2,1,0:T(8,128)}, f32[4,4,4,48,384]{4,3,2,1,0:T(8,128)}, f32[4,16,48,384]{3,2,1,0:T(8,128)}) custom-call(f32[3,16,16,384]{3,2,1,0:T(8,128)} %bitcast.11, f32[16,48,384]{2,1,0:T(8,128)} %bitcast.12), custom_call_target="tpu_custom_call" | custom-call | tf_op jit(solution)/shard_map/bcast/pallas_call | solution.py:373
  96.0 0.0 copy-done.1
  96.0 15.2 %pack.1 = f32[256,128,128]{2,1,0:T(8,128)} custom-call(s32[128]{0:T(128)} %copy-done.1, f32[128,128,128]{2,1,0:T(8,128)} %tiles_ref.1, s32[128,128]{1,0:T(8,128)} %rows_ref.1), custom_call_target="tpu_custom_call" | custom-call | tf_op jit(solution)/shard_map/pack/pallas_call | solution.py:78
  111.2 0.0 all-to-all-done
  111.2 12.1 %all-to-all-start.1 = ((f32[128,2,128,128]{3,2,1,0:T(8,128)}), f32[128,2,128,128]{3,2,1,0:T(8,128)}, u32[]{:S(2)}, u32[]{:S(2)}) async-start(f32[128,2,128,128]{3,2,1,0:T(8,128)} %bitcast.10), calls=%async_computation.1 | async-start | bytes 33554432 | tf_op jit(solution)/shard_map/all_to_all | solution.py:679
  123.3 0.6 pad_add_fusion.place_ref
  123.9 93.0 %chol.1 = (f32[1536,1536]{1,0:T(8,128)}, f32[1536,128]{1,0:T(8,128)}) custom-call(f32[3,4,2,256,384]{4,3,2,1,0:T(8,128)} %bitcast.13), custom_call_target="tpu_custom_call" | custom-call | flops 60000002048 | bytes 20000000 | tf_op jit(solution)/shard_map/chol/pallas_call | solution.py:511
  217.0 44.8 %solve.1 = (f32[768,384]{1,0:T(8,128)}, f32[768,768]{1,0:T(8,128)}) custom-call(s32[2]{0:T(128)} %pad_add_fusion.place_ref, f32[1536,1536]{1,0:T(8,128)} %get-tuple-element.13.l_ref, f32[1536,128]{1,0:T(8,128)} %get-tuple-element.14.w_ref, f32[768,384]{1,0:T(8,128)} %own_ref.1, f32[4,768,384]{2,1,0:T(8,128)} %bitcast.15, f32[4,768,384]{2,1,0:T(8,128)} %bitcast.14, ...), custom_call_target="tpu_custom_call" | custom-call | flops 30000001024 | bytes 30000000 | tf_op jit(solution)/shard_map/solve/pallas_call | solution.py:603
  261.8 0.6 broadcast.23
  262.4 0.8 reduce.3
  263.2 0.1 reshape.55.target_ref
  263.4 95.0 %all-to-all-done.1 = f32[128,2,128,128]{3,2,1,0:T(8,128)} async-done(((f32[128,2,128,128]{3,2,1,0:T(8,128)}), f32[128,2,128,128]{3,2,1,0:T(8,128)}, u32[]{:S(2)}, u32[]{:S(2)}) %all-to-all-start.1) | async-done | bytes 16777248 | tf_op jit(solution)/shard_map/all_to_all | solution.py:679
  358.4 0.0 copy-start
  358.4 1.7 copy-done
  360.0 14.5 %extend_add.1 = f32[768,768]{1,0:T(8,128)} custom-call(s32[256]{0:T(256)S(1)} %reshape.55.target_ref, f32[256,128,128]{2,1,0:T(8,128)} %bitcast.9.tiles_ref, f32[768,768]{1,0:T(8,128)S(1)} %copy-done), custom_call_target="tpu_custom_call" | custom-call | tf_op jit(solution)/shard_map/extend_add/pallas_call | solution.py:645
  (1 shorter events, 0.0 us)
Async XLA Ops:
  2.2 93.8 %copy-start.1 = (s32[128]{0:T(128)}, s32[128]{0:T(128)S(1)}, u32[]{:S(2)}) copy-start(s32[128]{0:T(128)S(1)} %get-tuple-element.20.dst_ref) | copy-start | bytes 1540
  3.1 108.1 %all-to-all-start = ((s32[128,1,2]{2,1,0:T(1,128)}), s32[128,1,2]{2,1,0:T(1,128)S(1)}, u32[]{:S(2)}, u32[]{:S(2)}) async-start(s32[128,1,2]{2,1,0:T(1,128)} %bitcast.7), calls=%async_computation | async-start | bytes 131072 | tf_op jit(solution)/shard_map/all_to_all | solution.py:674
  111.2 247.2 %all-to-all-start.1 = ((f32[128,2,128,128]{3,2,1,0:T(8,128)}), f32[128,2,128,128]{3,2,1,0:T(8,128)}, u32[]{:S(2)}, u32[]{:S(2)}) async-start(f32[128,2,128,128]{3,2,1,0:T(8,128)} %bitcast.10), calls=%async_computation.1 | async-start | bytes 33554432 | tf_op jit(solution)/shard_map/all_to_all | solution.py:679
  358.4 1.7 copy-start

commit v3 on v2

--- a/solution.py
+++ b/solution.py
@@ -1,3 +1,5 @@
+import functools
+
 import jax
 import jax.numpy as jnp
 from jax import lax
@@ -13,6 +15,8 @@
 F32 = jnp.float32
 BF16 = jnp.bfloat16
 BIG = 60 << 20
+PER = 32
+ORDERS = (("z", "x", "y"), ("x", "y", "z"), ("y", "z", "x"))
 
 
 def dot_nt(a, b):
@@ -74,7 +78,7 @@
 
 def pack(dst, tiles, rows, slots):
     count = tiles.shape[0]
-    per = 8
+    per = PER
     return pl.pallas_call(
         pack_kernel,
         grid_spec=pltpu.PrefetchScalarGridSpec(
@@ -95,7 +99,7 @@
     )(dst, tiles, rows)
 
 
-def bcast_kernel(pa_ref, pc_ref, ga_ref, gc_ref, gr_ref,
+def bcast_kernel(pa_ref, pc_ref, pt_ref, ga_ref, gc_ref, gr_ref, gt_ref,
                  s1a, s1c, r1a, r1c, loc, ss, rs, fs, fr, xs, xr):
     row = lax.axis_index("row")
     y = lax.axis_index("col")
@@ -203,34 +207,52 @@
                 send_c(q).start()
 
     chains = []
-    for s, order in enumerate((("z", "x", "y"), ("x", "y", "z"), ("y", "z", "x"))):
+    for s, order in enumerate(ORDERS):
         chains.append(("a", s, order))
     for s, order in enumerate((("z", "x"), ("x", "z"))):
         chains.append(("c", s, order))
     chains.append(("r", 0, ("y",)))
+    chains.append(("t", 0, ("z", "x", "y")))
+    shared = [n for n in range(len(chains)) if chains[n][0] != "r"]
     total = len(chains)
 
-    def block(kind, s, order, t, p, half=None):
+    def block(kind, s, order, t, p, half=None, cut=None):
         ind = {}
         for j, a in enumerate(order):
             ind[a] = slice(None) if j < t else (p if j == t else pos[a])
+        if cut is not None and kind != "r":
+            ind[order[0]] = cut
         if kind == "a":
             tail = () if half is None else (pl.ds(8 * half, 8), slice(None))
             fill = () if half is None else tail
             return ga_ref.at[(s, ind["y"], core, ind["x"], ind["z"]) + fill]
         if kind == "r":
-            return gr_ref.at[p] if half is None else gr_ref.at[p, pl.ds(8 * half, 8)]
+            first, size = (0, 16) if half is None else (8 * half, 8)
+            if cut is not None:
+                size = size // 4
+                first = first + cut * size
+            return gr_ref.at[p, pl.ds(first, size)]
+        if kind == "t":
+            fill = () if half is None else (pl.ds(8 * half, 8), slice(None))
+            return gt_ref.at[(ind["y"], core, ind["x"], ind["z"]) + fill]
         fill = () if half is None else (pl.ds(24 * half, 24), slice(None))
         return gc_ref.at[(2 * core + s, ind["x"], ind["z"]) + fill]
 
     sibling = (xz * 2 + (1 - core), y)
 
-    def near(n, t, up):
+    def cuts(n, t):
+        if chains[n][0] == "t":
+            return (None,)
+        return range(4) if t > 0 or chains[n][0] == "r" else (None,)
+
+    def near(n, t, up, cut=None):
         kind, s, order = chains[n]
         a = order[t]
         p = pos[a]
-        b = block(kind, s, order, t, p)
-        src = pc_ref if kind == "r" else b
+        b = block(kind, s, order, t, p, None, cut)
+        src = b
+        if kind == "r":
+            src = pc_ref if cut is None else pc_ref.at[pl.ds(cut * 4, 4)]
         return remote(src, b, ss.at[n, t, up], rs.at[n, t, up],
                       device(a, lax.rem(p + (1 if up else 3), 4)))
 
@@ -240,11 +262,11 @@
         b = block(kind, s, order, t, lax.rem(pos[a] + (3 if up else 1), 4))
         remote(b, b, ss.at[n, t, up], rs.at[n, t, up], (row, y)).wait_recv()
 
-    def far(n, t, up):
+    def far(n, t, up, cut=None):
         kind, s, order = chains[n]
         a = order[t]
         p = pos[a]
-        b = block(kind, s, order, t, lax.rem(p + (3 if up else 1), 4), 0 if up else 1)
+        b = block(kind, s, order, t, lax.rem(p + (3 if up else 1), 4), 0 if up else 1, cut)
         return remote(b, b, fs.at[n, t, up], fr.at[n, t, up],
                       device(a, lax.rem(p + (1 if up else 3), 4)))
 
@@ -254,10 +276,10 @@
         b = block(kind, s, order, t, lax.rem(pos[a] + 2, 4), 0 if up else 1)
         remote(b, b, fs.at[n, t, up], fr.at[n, t, up], (row, y)).wait_recv()
 
-    def cross(n, shift):
+    def cross(n, shift, cut=None):
         kind, s, order = chains[n]
         t = len(order) - 1
-        b = block(kind, s, order, t, lax.rem(pos[order[t]] + shift, 4))
+        b = block(kind, s, order, t, lax.rem(pos[order[t]] + shift, 4), None, cut)
         return remote(b, b, xs.at[n, shift], xr.at[n, shift], sibling)
 
     def cross_wait(n, shift):
@@ -268,13 +290,18 @@
             ind[a] = slice(None) if j < t else lax.rem(pos[a] + shift, 4)
         if kind == "a":
             b = ga_ref.at[s, ind["y"], 1 - core, ind["x"], ind["z"]]
+        elif kind == "t":
+            b = gt_ref.at[ind["y"], 1 - core, ind["x"], ind["z"]]
         else:
             b = gc_ref.at[2 * (1 - core) + s, ind["x"], ind["z"]]
         remote(b, b, xs.at[n, shift], xr.at[n, shift], (row, y)).wait_recv()
 
-    diag, column, own = (0, 1, 2), (3, 4), (5,)
+    diag, column, own = (6, 0, 1, 2), (3, 4), (5,)
+    table = pltpu.make_async_copy(pt_ref, gt_ref.at[y, core, x, z], loc.at[2])
+    table.start()
     for up in range(2):
-        near(5, 0, up).start()
+        for cut in cuts(5, 0):
+            near(5, 0, up, cut).start()
     @pl.when(is_a)
     def _():
         s, d = piece_a(0)
@@ -284,19 +311,25 @@
     def _():
         s = pa_ref.at[:, 0]
         remote(s, ga_ref.at[:, y, core, x, z], s1a.at[0], r1a.at[0], (row, y)).wait_recv()
+
+    def share(n, shift):
+        for cut in (None,) if chains[n][0] == "t" else range(4):
+            cross(n, shift, cut).start()
 
     def begin(ns, t):
         for n in ns:
             for up in range(2):
-                near(n, t, up).start()
+                for cut in cuts(n, t):
+                    near(n, t, up, cut).start()
 
     def forward(ns, t):
         for n in ns:
             for up in range(2):
                 near_wait(n, t, up)
-                far(n, t, up).start()
-                if n < 5 and t == len(chains[n][2]) - 1:
-                    cross(n, 3 if up else 1).start()
+                for cut in cuts(n, t):
+                    far(n, t, up, cut).start()
+                if n in shared and t == len(chains[n][2]) - 1:
+                    share(n, 3 if up else 1)
 
     def settle(n, t):
         for up in range(2):
@@ -307,13 +340,14 @@
             settle(n, t)
             begin([n], t + 1)
             if t + 1 == len(chains[n][2]) - 1:
-                cross(n, 0).start()
+                share(n, 0)
 
     def finish(ns, t):
         for n in ns:
             settle(n, t)
-            cross(n, 2).start()
-
+            share(n, 2)
+
+    table.wait()
     begin(diag, 0)
     for h in range(2):
         yy = 2 * core + h
@@ -340,7 +374,7 @@
     forward(diag, 2)
     finish(diag, 2)
     settle(5, 0)
-    for n in range(5):
+    for n in shared:
         for shift in range(4):
             cross_wait(n, shift)
     for n in range(total):
@@ -348,7 +382,7 @@
             for up in range(2):
                 near(n, t, up).wait_send()
                 far(n, t, up).wait_send()
-    for n in range(5):
+    for n in shared:
         for shift in range(4):
             cross(n, shift).wait_send()
 
@@ -367,26 +401,27 @@
                 send_c(q).wait_send()
 
 
-def bcast(panel):
+def bcast(panel, table):
     rows, cols = panel.shape
     dma = pltpu.SemaphoreType.DMA
     return pl.pallas_call(
         bcast_kernel,
-        in_specs=[pl.BlockSpec(memory_space=pl.ANY)] * 2,
-        out_specs=[pl.BlockSpec(memory_space=pl.ANY)] * 3,
+        in_specs=[pl.BlockSpec(memory_space=pl.ANY)] * 3,
+        out_specs=[pl.BlockSpec(memory_space=pl.ANY)] * 4,
         out_shape=[
             jax.ShapeDtypeStruct((3, 4, 2, 4, 4, 16, cols), F32),
             jax.ShapeDtypeStruct((4, 4, 4, 48, cols), F32),
             jax.ShapeDtypeStruct((4, 16, 48, cols), F32),
+            jax.ShapeDtypeStruct((4, 2, 4, 4) + table.shape, F32),
         ],
         scratch_shapes=[
-            dma((16,)), dma((16,)), dma((1,)), dma((2,)), dma((2,)),
-            dma((6, 3, 2)), dma((6, 3, 2)), dma((6, 3, 2)), dma((6, 3, 2)),
-            dma((5, 4)), dma((5, 4)),
+            dma((16,)), dma((16,)), dma((1,)), dma((2,)), dma((3,)),
+            dma((7, 3, 2)), dma((7, 3, 2)), dma((7, 3, 2)), dma((7, 3, 2)),
+            dma((7, 4)), dma((7, 4)),
         ],
         compiler_params=pltpu.CompilerParams(has_side_effects=True, collective_id=0),
         name="bcast",
-    )(panel.reshape(3, 16, 16, cols), panel.reshape(16, 48, cols))
+    )(panel.reshape(3, 16, 16, cols), panel.reshape(16, 48, cols), table)
 
 
 def wide(v):
@@ -621,42 +656,58 @@
     )(place, factor, inverse, own, mine, theirs, trailing)
 
 
-def add_kernel(target_ref, tiles_ref, base_ref, out_ref):
+def add_kernel(target_ref, *refs):
+    *tile_refs, base_ref, out_ref, total = refs
     step = pl.program_id(0)
-    per = tiles_ref.shape[0]
+    streams = len(tile_refs)
+    per = streams * tile_refs[0].shape[0]
+    rows = out_ref.shape[0]
     tile_cols = out_ref.shape[1] // TB
 
     @pl.when(step == 0)
     def _():
-        out_ref[...] = base_ref[...]
-
+        total[0:rows, :] = base_ref[...]
+
+    spare = (rows // TB) * tile_cols
     for i in range(per):
-        target = target_ref[step * per + i]
-
-        @pl.when(target >= 0)
-        def _():
-            r = pl.ds(pl.multiple_of(lax.div(target, tile_cols) * TB, TB), TB)
-            c = pl.ds(pl.multiple_of(lax.rem(target, tile_cols) * TB, TB), TB)
-            out_ref[r, c] = out_ref[r, c] + tiles_ref[i]
+        sizes = per // streams
+        at = (i % streams) * (pl.num_programs(0) * sizes) + step * sizes + i // streams
+        target = target_ref[at]
+        target = jnp.where(target < 0, spare, target)
+        r = pl.ds(pl.multiple_of(lax.div(target, tile_cols) * TB, TB), TB)
+        c = pl.ds(pl.multiple_of(lax.rem(target, tile_cols) * TB, TB), TB)
+        total[r, c] = total[r, c] + tile_refs[i % streams][i // streams]
+
+    @pl.when(step == pl.num_programs(0) - 1)
+    def _():
+        out_ref[...] = total[0:rows, :]
+
+
+def stream_block(first, i, t):
+    return (first + i, 0, 0)
 
 
 def extend_add(target, tiles, base):
-    per = 16
+    streams, size = 4, 8
+    steps = tiles.shape[0] // (streams * size)
     return pl.pallas_call(
         add_kernel,
         grid_spec=pltpu.PrefetchScalarGridSpec(
             num_scalar_prefetch=1,
-            grid=(tiles.shape[0] // per,),
+            grid=(steps,),
             in_specs=[
-                pl.BlockSpec((per, TB, TB), lambda i, t: (i, 0, 0)),
+                pl.BlockSpec((size, TB, TB), functools.partial(stream_block, s * steps))
+                for s in range(streams)
+            ] + [
                 pl.BlockSpec(base.shape, lambda i, t: (0, 0)),
             ],
             out_specs=pl.BlockSpec(base.shape, lambda i, t: (0, 0)),
+            scratch_shapes=[pltpu.VMEM((base.shape[0] + TB, base.shape[1]), F32)],
         ),
         out_shape=jax.ShapeDtypeStruct(base.shape, F32),
-        compiler_params=pltpu.CompilerParams(vmem_limit_bytes=32 << 20),
+        compiler_params=pltpu.CompilerParams(vmem_limit_bytes=40 << 20),
         name="extend_add",
-    )(target, tiles, base)
+    )(target, *([tiles] * streams), base)
 
 
 def body(panel, trailing, child_tiles, child_owner, child_tile, child_rows):
@@ -671,14 +722,17 @@
     slots = devices * cap
     hit = dst[:, None] == jnp.arange(slots, dtype=jnp.int32)[None, :]
     target = (jnp.sum(jnp.where(hit, child_tile[:, None] + 1, 0), axis=0) - 1).astype(jnp.int32)
-    got_target = lax.all_to_all(
-        target.reshape(devices, cap), both, split_axis=0, concat_axis=0, tiled=True)
+    table = jnp.pad(target.reshape(devices, cap).T.astype(F32), ((0, 14), (0, 0)))
     packed = pack(dst, child_tiles, child_rows, slots)
-    ga, gc, mine = bcast(panel)
+    ga, gc, mine, tables = bcast(panel, table)
     packed, ga = lax.optimization_barrier((packed, ga))
     got = lax.all_to_all(
         packed.reshape(devices, cap, TB, TB), both, split_axis=0, concat_axis=0, tiled=True)
     row_index, col_index = lax.axis_index("row"), lax.axis_index("col")
+    me = row_index * lax.axis_size("col") + col_index
+    lane = jnp.arange(devices, dtype=jnp.int32)
+    picked = jnp.sum(jnp.where(lane == me, tables[..., :cap, :], 0.0), axis=-1)
+    got_target = picked.transpose(2, 3, 1, 0, 4).astype(jnp.int32)
     factor, inverse = chol(ga.reshape(3, 4, 2, 256, panel.shape[1]))
     place = jnp.stack([row_index, col_index]).astype(jnp.int32)
     factor_panel, base = solve(

time: 375 us -> 360 us (0.960)
  starting transfers between devices: 22.4 us -> 12.6 us
  Pallas kernels: 250 us -> 246 us
    all_to_all x1 -> x0, starting transfers between devices: 10.3 us -> none  [body(): lax.all_to_all(target.reshape(devices, cap), both, split_axis=0, concat_a...]
    pallas_call x1, Pallas kernels: 15.2 us -> 10.2 us  [pack(): pl.pallas_call(pack_kernel, grid_spec=pltpu.PrefetchScalarGridSpec(num_sc...]
    pallas_call x1, Pallas kernels: 82.6 us -> 87.2 us  [bcast(): pl.pallas_call(bcast_kernel, in_specs=[pl.BlockSpec(memory_space=pl.ANY)]...]
    pallas_call x1, Pallas kernels: 14.5 us -> 10.6 us  [extend_add(): pl.pallas_call(add_kernel, grid_spec=pltpu.PrefetchScalarGridSpec(num_sca...]
  transfers between devices with their start and end apart: 2 -> 1, of which waited for: 1 -> 1; matrix products, arithmetic and copies ran while one was open for 1% -> 1% of each run, Pallas kernels for 63% -> 38%
where the time goes in v3:
time: 360 us; the launch traced here: 359 us
  Pallas kernels  246 us (68%)
  waiting for transfers between devices  93.6 us (26%)
  starting transfers between devices  12.6 us (4%)
    all_to_all x1, waiting for transfers between devices, body(): lax.all_to_all(packed.reshape(devices, cap, TB, TB), both, split_axis=0,...  93.6 us
    pallas_call x1, Pallas kernels, chol(): pl.pallas_call(chol_kernel, out_shape=[jax.ShapeDtypeStruct((PW, PW), F32...  93.1 us
    pallas_call x1, Pallas kernels, bcast(): pl.pallas_call(bcast_kernel, in_specs=[pl.BlockSpec(memory_space=pl.ANY)]...  87.2 us
    pallas_call x1, Pallas kernels, solve(): pl.pallas_call(solve_kernel, in_specs=[smem] + [vmem] * 6, out_specs=[vme...  44.8 us
    all_to_all x1, starting transfers between devices, body(): lax.all_to_all(packed.reshape(devices, cap, TB, TB), both, split_axis=0,...  12.6 us
    pallas_call x1, Pallas kernels, extend_add(): pl.pallas_call(add_kernel, grid_spec=pltpu.PrefetchScalarGridSpec(num_sca...  10.6 us
    pallas_call x1, Pallas kernels, pack(): pl.pallas_call(pack_kernel, grid_spec=pltpu.PrefetchScalarGridSpec(num_sc...  10.2 us
  transfers between devices with their start and end apart: 1, of which 1 were waited for; matrix products, arithmetic and copies ran while one was open for 1% of the time, Pallas kernels for 38%

profile of v3, /device:TPU:26, one launch (start us, length us, event | category | flops | bytes accessed | tf_op | source)
XLA Modules:
  0.0 359.1 jit_solution(1426943745420393724)
XLA Ops:
  0.6 0.9 select_reduce_fusion.2
  1.5 0.7 multiply_add_fusion
  2.2 0.0 copy-start.1
  2.2 0.1 select_reduce_fusion.1
  2.3 0.1 convert_element_type.18
  2.5 0.1 copy.11
  2.5 0.6 pad.4.pt_ref
  3.2 0.0 copy-done.1
  3.2 10.2 %pack.1 = f32[256,128,128]{2,1,0:T(8,128)} custom-call(s32[128]{0:T(128)} %copy-done.1, f32[128,128,128]{2,1,0:T(8,128)} %tiles_ref.1, s32[128,128]{1,0:T(8,128)} %rows_ref.1), custom_call_target="tpu_custom_call" | custom-call | tf_op jit(solution)/shard_map/pack/pallas_call | solution.py:82
  13.4 87.2 %bcast.1 = (f32[3,4,2,4,4,16,384]{6,5,4,3,2,1,0:T(8,128)}, f32[4,4,4,48,384]{4,3,2,1,0:T(8,128)}, f32[4,16,48,384]{3,2,1,0:T(8,128)}, f32[4,2,4,4,16,128]{5,4,3,2,1,0:T(8,128)}) custom-call(f32[3,16,16,384]{3,2,1,0:T(8,128)} %bitcast.13, f32[16,48,384]{2,1,0:T(8,128)} %bitcast.14, f32[16,128]{1,0:T(8,128)} %pad.4.pt_ref), custom_call_target="tpu_custom_call" | custom-call | tf_op jit(solution)/shard_map/bcast/pallas_call | solution.py:407
  100.6 12.6 %all-to-all-start = ((f32[128,2,128,128]{3,2,1,0:T(8,128)}), f32[128,2,128,128]{3,2,1,0:T(8,128)}, u32[]{:S(2)}, u32[]{:S(2)}) async-start(f32[128,2,128,128]{3,2,1,0:T(8,128)} %bitcast.12), calls=%async_computation | async-start | bytes 33554432 | tf_op jit(solution)/shard_map/all_to_all | solution.py:729
  113.2 1.3 select_reduce_fusion
  114.6 0.1 reshape.43.target_ref
  114.7 0.6 pad_add_fusion.place_ref
  115.3 93.1 %chol.1 = (f32[1536,1536]{1,0:T(8,128)}, f32[1536,128]{1,0:T(8,128)}) custom-call(f32[3,4,2,256,384]{4,3,2,1,0:T(8,128)} %bitcast.16), custom_call_target="tpu_custom_call" | custom-call | flops 60000002048 | bytes 20000000 | tf_op jit(solution)/shard_map/chol/pallas_call | solution.py:546
  208.4 44.8 %solve.1 = (f32[768,384]{1,0:T(8,128)}, f32[768,768]{1,0:T(8,128)}) custom-call(s32[2]{0:T(128)} %pad_add_fusion.place_ref, f32[1536,1536]{1,0:T(8,128)} %get-tuple-element.14.l_ref, f32[1536,128]{1,0:T(8,128)} %get-tuple-element.15.w_ref, f32[768,384]{1,0:T(8,128)} %own_ref.1, f32[4,768,384]{2,1,0:T(8,128)} %bitcast.18, f32[4,768,384]{2,1,0:T(8,128)} %bitcast.17, ...), custom_call_target="tpu_custom_call" | custom-call | flops 30000001024 | bytes 30000000 | tf_op jit(solution)/shard_map/solve/pallas_call | solution.py:638
  253.3 93.6 %all-to-all-done = f32[128,2,128,128]{3,2,1,0:T(8,128)} async-done(((f32[128,2,128,128]{3,2,1,0:T(8,128)}), f32[128,2,128,128]{3,2,1,0:T(8,128)}, u32[]{:S(2)}, u32[]{:S(2)}) %all-to-all-start) | async-done | bytes 16777248 | tf_op jit(solution)/shard_map/all_to_all | solution.py:729
  346.9 0.0 copy-start
  346.9 1.7 copy-done
  348.6 10.6 %extend_add.1 = f32[768,768]{1,0:T(8,128)} custom-call(s32[256]{0:T(256)S(1)} %reshape.43.target_ref, f32[256,128,128]{2,1,0:T(8,128)} %bitcast.10.refs_0_.refs_1_.refs_2_.refs_3_, f32[256,128,128]{2,1,0:T(8,128)} %bitcast.10.refs_0_.refs_1_.refs_2_.refs_3_, f32[256,128,128]{2,1,0:T(8,128)} %bitcast.10.refs_0_.refs_1_.refs_2_.refs_3_, ...), custom_call_target="tpu_custom_call" | custom-call | tf_op jit(solution)/shard_map/extend_add/pallas_call | solution.py:693
  (4 shorter events, 0.1 us)
Async XLA Ops:
  2.2 1.0 copy-start.1
  100.6 246.3 %all-to-all-start = ((f32[128,2,128,128]{3,2,1,0:T(8,128)}), f32[128,2,128,128]{3,2,1,0:T(8,128)}, u32[]{:S(2)}, u32[]{:S(2)}) async-start(f32[128,2,128,128]{3,2,1,0:T(8,128)} %bitcast.12), calls=%async_computation | async-start | bytes 33554432 | tf_op jit(solution)/shard_map/all_to_all | solution.py:729
  346.9 1.7 copy-start

commit v4 on v3

--- a/solution.py
+++ b/solution.py
@@ -366,11 +366,11 @@
     forward(column, 0)
     advance(diag, 0)
     advance(column, 0)
+    forward(own, 0)
     forward(diag, 1)
     forward(column, 1)
     advance(diag, 1)
     finish(column, 1)
-    forward(own, 0)
     forward(diag, 2)
     finish(diag, 2)
     settle(5, 0)

time: 360 us -> 352 us (0.978)
  Pallas kernels: 246 us -> 238 us
    pallas_call x1, Pallas kernels: 87.2 us -> 79.7 us  [bcast(): pl.pallas_call(bcast_kernel, in_specs=[pl.BlockSpec(memory_space=pl.ANY)]...]
  transfers between devices with their start and end apart: 1 -> 1, of which waited for: 1 -> 1; matrix products, arithmetic and copies ran while one was open for 1% -> 1% of each run, Pallas kernels for 38% -> 39%
where the time goes in v4:
time: 352 us; the launch traced here: 351 us
  Pallas kernels  238 us (68%)
  waiting for transfers between devices  93.6 us (27%)
  starting transfers between devices  12.4 us (4%)
  other arithmetic  3.59 us (1%)
    all_to_all x1, waiting for transfers between devices, body(): lax.all_to_all(packed.reshape(devices, cap, TB, TB), both, split_axis=0,...  93.6 us
    pallas_call x1, Pallas kernels, chol(): pl.pallas_call(chol_kernel, out_shape=[jax.ShapeDtypeStruct((PW, PW), F32...  93.1 us
    pallas_call x1, Pallas kernels, bcast(): pl.pallas_call(bcast_kernel, in_specs=[pl.BlockSpec(memory_space=pl.ANY)]...  79.7 us
    pallas_call x1, Pallas kernels, solve(): pl.pallas_call(solve_kernel, in_specs=[smem] + [vmem] * 6, out_specs=[vme...  44.8 us
    all_to_all x1, starting transfers between devices, body(): lax.all_to_all(packed.reshape(devices, cap, TB, TB), both, split_axis=0,...  12.4 us
    pallas_call x1, Pallas kernels, extend_add(): pl.pallas_call(add_kernel, grid_spec=pltpu.PrefetchScalarGridSpec(num_sca...  10.6 us
    pallas_call x1, Pallas kernels, pack(): pl.pallas_call(pack_kernel, grid_spec=pltpu.PrefetchScalarGridSpec(num_sc...  10.2 us
  transfers between devices with their start and end apart: 1, of which 1 were waited for; matrix products, arithmetic and copies ran while one was open for 1% of the time, Pallas kernels for 39%

profile of v4, /device:TPU:26, one launch (start us, length us, event | category | flops | bytes accessed | tf_op | source)
XLA Modules:
  0.0 351.5 jit_solution(13488063154288910238)
XLA Ops:
  0.6 0.9 select_reduce_fusion.2
  1.5 0.7 multiply_add_fusion
  2.2 0.0 copy-start.1
  2.2 0.1 select_reduce_fusion.1
  2.3 0.1 convert_element_type.18
  2.5 0.1 copy.11
  2.5 0.6 pad.4.pt_ref
  3.2 0.0 copy-done.1
  3.2 10.2 %pack.1 = f32[256,128,128]{2,1,0:T(8,128)} custom-call(s32[128]{0:T(128)} %copy-done.1, f32[128,128,128]{2,1,0:T(8,128)} %tiles_ref.1, s32[128,128]{1,0:T(8,128)} %rows_ref.1), custom_call_target="tpu_custom_call" | custom-call | tf_op jit(solution)/shard_map/pack/pallas_call | solution.py:82
  13.4 79.7 %bcast.1 = (f32[3,4,2,4,4,16,384]{6,5,4,3,2,1,0:T(8,128)}, f32[4,4,4,48,384]{4,3,2,1,0:T(8,128)}, f32[4,16,48,384]{3,2,1,0:T(8,128)}, f32[4,2,4,4,16,128]{5,4,3,2,1,0:T(8,128)}) custom-call(f32[3,16,16,384]{3,2,1,0:T(8,128)} %bitcast.13, f32[16,48,384]{2,1,0:T(8,128)} %bitcast.14, f32[16,128]{1,0:T(8,128)} %pad.4.pt_ref), custom_call_target="tpu_custom_call" | custom-call | tf_op jit(solution)/shard_map/bcast/pallas_call | solution.py:407
  93.1 12.4 %all-to-all-start = ((f32[128,2,128,128]{3,2,1,0:T(8,128)}), f32[128,2,128,128]{3,2,1,0:T(8,128)}, u32[]{:S(2)}, u32[]{:S(2)}) async-start(f32[128,2,128,128]{3,2,1,0:T(8,128)} %bitcast.12), calls=%async_computation | async-start | bytes 33554432 | tf_op jit(solution)/shard_map/all_to_all | solution.py:729
  105.6 1.3 select_reduce_fusion
  106.9 0.1 reshape.43.target_ref
  107.1 0.6 pad_add_fusion.place_ref
  107.7 93.1 %chol.1 = (f32[1536,1536]{1,0:T(8,128)}, f32[1536,128]{1,0:T(8,128)}) custom-call(f32[3,4,2,256,384]{4,3,2,1,0:T(8,128)} %bitcast.16), custom_call_target="tpu_custom_call" | custom-call | flops 60000002048 | bytes 20000000 | tf_op jit(solution)/shard_map/chol/pallas_call | solution.py:546
  200.8 44.8 %solve.1 = (f32[768,384]{1,0:T(8,128)}, f32[768,768]{1,0:T(8,128)}) custom-call(s32[2]{0:T(128)} %pad_add_fusion.place_ref, f32[1536,1536]{1,0:T(8,128)} %get-tuple-element.14.l_ref, f32[1536,128]{1,0:T(8,128)} %get-tuple-element.15.w_ref, f32[768,384]{1,0:T(8,128)} %own_ref.1, f32[4,768,384]{2,1,0:T(8,128)} %bitcast.18, f32[4,768,384]{2,1,0:T(8,128)} %bitcast.17, ...), custom_call_target="tpu_custom_call" | custom-call | flops 30000001024 | bytes 30000000 | tf_op jit(solution)/shard_map/solve/pallas_call | solution.py:638
  245.6 93.6 %all-to-all-done = f32[128,2,128,128]{3,2,1,0:T(8,128)} async-done(((f32[128,2,128,128]{3,2,1,0:T(8,128)}), f32[128,2,128,128]{3,2,1,0:T(8,128)}, u32[]{:S(2)}, u32[]{:S(2)}) %all-to-all-start) | async-done | bytes 16777248 | tf_op jit(solution)/shard_map/all_to_all | solution.py:729
  339.2 0.0 copy-start
  339.2 1.7 copy-done
  340.9 10.6 %extend_add.1 = f32[768,768]{1,0:T(8,128)} custom-call(s32[256]{0:T(256)S(1)} %reshape.43.target_ref, f32[256,128,128]{2,1,0:T(8,128)} %bitcast.10.refs_0_.refs_1_.refs_2_.refs_3_, f32[256,128,128]{2,1,0:T(8,128)} %bitcast.10.refs_0_.refs_1_.refs_2_.refs_3_, f32[256,128,128]{2,1,0:T(8,128)} %bitcast.10.refs_0_.refs_1_.refs_2_.refs_3_, ...), custom_call_target="tpu_custom_call" | custom-call | tf_op jit(solution)/shard_map/extend_add/pallas_call | solution.py:693
  (4 shorter events, 0.1 us)
Async XLA Ops:
  2.2 1.0 copy-start.1
  93.1 246.1 %all-to-all-start = ((f32[128,2,128,128]{3,2,1,0:T(8,128)}), f32[128,2,128,128]{3,2,1,0:T(8,128)}, u32[]{:S(2)}, u32[]{:S(2)}) async-start(f32[128,2,128,128]{3,2,1,0:T(8,128)} %bitcast.12), calls=%async_computation | async-start | bytes 33554432 | tf_op jit(solution)/shard_map/all_to_all | solution.py:729
  339.2 1.7 copy-start
